TPU v7x, 256 devices: a whole 4x4x8 slice. The times are simulated.
256 devices in a mesh: dp: 2 (over z_lo), chan: 8 (over z_hi, core), seq: 16 (over y, x).
Axes of the slice: x: 4, y: 4, z: 8 (z_hi: 4, z_lo: 2; z = z_hi * 2 + z_lo), core: 2. Of those that a mesh axis runs over, the one named last changes fastest.
Arguments:
- query_proj: bfloat16 [2, 2048, 8192], P('dp', 'chan', 'seq'), may hold values from -6 to 6
- key_proj: bfloat16 [2, 2048, 8192], P('dp', 'chan', 'seq'), may hold values from -6 to 6
- value_proj: bfloat16 [2, 2048, 8192], P('dp', 'chan', 'seq'), may hold values from -6 to 6
- grad_out: bfloat16 [2, 2048, 8192], P('dp', 'chan', 'seq'), may hold values from -6 to 6
- out_weight: bfloat16 [2048, 2048], P('chan'), may hold values from -0.125 to 0.125
- long_filter: float32 [2048, 8192], P(('chan', 'seq')), may hold values from -2 to 2, as said below
Outputs:
- grad_query: bfloat16 [2, 2048, 8192], P('dp', 'chan', 'seq')
- grad_key: bfloat16 [2, 2048, 8192], P('dp', 'chan', 'seq')
- grad_value: bfloat16 [2, 2048, 8192], P('dp', 'chan', 'seq')
- grad_weight: float32 [2048, 2048], P('chan')
Inputs may be any that keep to these rules, and one draw needn't show every extreme that they name: `long_filter`: taps of each channel's causal filter.
All inputs are finite; a program needn't handle non-finite values.
Results may differ from a plain program's by a relative error of at most 0.0029.
Values may be sent and summed in bfloat16 or wider, within the bound.
No kernel may reach another device: no remote copies, remote signals or barrier semaphores. Data moves between devices by JAX's collectives and lax.ppermute only.
A program may use at most 64 MiB of HBM per device.

v0:
```python
import math

import jax
import jax.numpy as jnp
import ml_dtypes
import numpy as np
from jax import lax
from jax.experimental import pallas as pl
from jax.experimental.pallas import tpu as pltpu
from jax.sharding import PartitionSpec as P


WIDE = 128
TALL = 64
LIMIT = 20


def split_table(values):
    high = values.astype(ml_dtypes.bfloat16)
    low = (values - high.astype(np.float64)).astype(ml_dtypes.bfloat16)
    return high, low


def make_tables(row_of):
    freq = np.arange(TALL) + 0.25
    first = 2.0 * np.pi / TALL * freq[:, None] * np.asarray(row_of)[None, :]
    first = np.concatenate([np.cos(first), -np.sin(first)], axis=0)
    high, low = split_table(first)
    analyse = np.concatenate([high, high, low], axis=1)
    last = 2.0 * np.pi / TALL * np.asarray(row_of)[:, None] * freq[None, :]
    last = np.concatenate([np.cos(last), -np.sin(last)], axis=1) / (TALL * WIDE)
    high, low = split_table(last)
    restore = np.concatenate([high, high, low], axis=1)
    return analyse, restore


def make_shared():
    freq = np.arange(TALL) + 0.25
    cols = np.arange(WIDE)
    turn = 2.0 * np.pi / (TALL * WIDE) * freq[:, None] * cols[None, :]
    twist = np.stack([np.cos(turn), np.sin(turn)]).astype(np.float32)
    angle = 2.0 * np.pi / WIDE * (cols[:, None] * cols[None, :] % WIDE)
    cos, sin = np.cos(angle), np.sin(angle)
    there = np.concatenate([np.concatenate([cos, -sin], 1), np.concatenate([sin, cos], 1)], 0)
    back = np.concatenate([np.concatenate([cos, sin], 1), np.concatenate([-sin, cos], 1)], 0)
    out = []
    for table in (there, back):
        high, low = split_table(table)
        out.append(np.concatenate([high, high, low], axis=0))
    return twist, out[0], out[1]


def halves(values):
    high = values.astype(jnp.bfloat16)
    low = (values - high.astype(jnp.float32)).astype(jnp.bfloat16)
    return high, low


def dot(left, right):
    return jnp.dot(left, right, preferred_element_type=jnp.float32)


def stacked(values):
    high, low = halves(values)
    return jnp.concatenate([high, low, high], axis=0)


def beside(values):
    high, low = halves(values)
    return jnp.concatenate([high, low, high], axis=1)


def forward_pair(pair, analyse, twist, there):
    both = dot(analyse, stacked(jnp.concatenate(pair, axis=1)))
    cos, sin = twist[0], twist[1]
    rows = []
    for which in range(2):
        real = both[:TALL, which * WIDE : (which + 1) * WIDE]
        imag = both[TALL:, which * WIDE : (which + 1) * WIDE]
        rows.append(jnp.concatenate([real * cos + imag * sin, imag * cos - real * sin], axis=1))
    return dot(beside(jnp.concatenate(rows, axis=0)), there)


def inverse_pair(spec, restore, twist, back):
    both = dot(beside(spec), back)
    cos, sin = twist[0], twist[1]
    columns = []
    for which in range(2):
        real = both[which * TALL : (which + 1) * TALL, :WIDE]
        imag = both[which * TALL : (which + 1) * TALL, WIDE:]
        columns.append(jnp.concatenate([real * cos - imag * sin, real * sin + imag * cos], axis=0))
    return dot(restore, stacked(jnp.concatenate(columns, axis=1)))


def filter_kernel(filt_ref, analyse_ref, twist_ref, there_ref, spec_ref):
    twist = twist_ref[...]
    for pair in range(filt_ref.shape[0] // 2):
        inputs = [filt_ref[2 * pair], filt_ref[2 * pair + 1]]
        spec_ref[pair] = forward_pair(inputs, analyse_ref[...], twist, there_ref[...])


def conv_kernel(conjugate, offset, signal_ref, spec_ref, analyse_ref, restore_ref, twist_ref, there_ref, back_ref, out_ref):
    twist = twist_ref[...]
    blocks, channels, width = out_ref.shape
    pieces = width // WIDE
    for pair in range(channels // 2):
        inputs = []
        for channel in (2 * pair, 2 * pair + 1):
            rows = signal_ref[:, channel, offset : offset + width]
            inputs.append(
                jnp.concatenate([rows[:, q * WIDE : (q + 1) * WIDE] for q in range(pieces)], axis=0)
            )
        spec = forward_pair(inputs, analyse_ref[...], twist, there_ref[...])
        real, imag = spec[:, :WIDE], spec[:, WIDE:]
        filt = spec_ref[pair]
        filt_real, filt_imag = filt[:, :WIDE], filt[:, WIDE:]
        if conjugate:
            filt_imag = -filt_imag
        product = jnp.concatenate(
            [real * filt_real - imag * filt_imag, real * filt_imag + imag * filt_real], axis=1
        )
        result = inverse_pair(product, restore_ref[...], twist, back_ref[...])
        for which in range(2):
            column = result[:, which * WIDE : (which + 1) * WIDE]
            row = jnp.concatenate([column[q * blocks : (q + 1) * blocks] for q in range(pieces)], axis=1)
            out_ref[:, 2 * pair + which, :] = row


def places(place_ref, step):
    chans = 8
    mine = place_ref[0]
    twin = mine + 1 - 2 * lax.rem(mine, 2)
    out = []
    for base in (mine, twin):
        for ahead in (0, chans - 2, 2):
            out.append((lax.rem(base + ahead, chans) * step, step))
        far = lax.rem(base + chans // 2, chans) * step
        out.append((far, step // 2))
        out.append((far + step // 2, step // 2))
    return out


def gate_kernel(place_ref, conv_ref, query_ref, weight_ref, *refs):
    blocks, (both_ref, mid_ref) = refs[:10], refs[10:]
    step = blocks[0].shape[0]
    total = None
    for (start, size), block in zip(places(place_ref, step), blocks):
        columns = weight_ref[:, pl.ds(pl.multiple_of(start, WIDE), size)]
        term = dot(columns, block[...])
        total = term if total is None else total + term
    mid_ref[...] = total
    seqs, rows, width = conv_ref.shape
    both_ref[:, :, :width] = conv_ref[...]
    gate = query_ref[...].astype(jnp.float32) * total
    both_ref[:, :, width:] = gate.reshape(seqs, rows, width)


def part_kernel(place_ref, both_ref, query_ref, *refs):
    blocks, (part_ref,) = refs[:10], refs[10:]
    step = blocks[0].shape[0]
    channels, width = query_ref.shape
    conv_out = both_ref[:, :, :width].reshape(channels, width)
    gated = (query_ref[...].astype(jnp.float32) * conv_out).astype(jnp.bfloat16)
    for (start, size), block in zip(places(place_ref, step), blocks):
        term = lax.dot_general(
            gated, block[...], (((1,), (1,)), ((), ())), preferred_element_type=jnp.float32
        )
        part_ref[:, pl.ds(pl.multiple_of(start, WIDE), size)] = term.astype(jnp.bfloat16)


def total_kernel(scale, part_ref, out_ref):
    group, rows, features = part_ref.shape
    half = features // 2
    total = part_ref[0].astype(jnp.float32)
    for source in range(1, group):
        total = total + part_ref[source].astype(jnp.float32)
    total = (total * scale).astype(jnp.bfloat16)
    out_ref[:rows, :] = total[:, :half]
    out_ref[rows:, :] = total[:, half:]


def last_kernel(mine_ref, other_ref, back_ref, out_ref):
    seqs, _, span = back_ref.shape
    rows = mine_ref.shape[0]
    for target in range(seqs):
        out_ref[target, :rows, :] = mine_ref[...]
        out_ref[target, rows : 2 * rows, :] = other_ref[...]
        high, low = halves(back_ref[target])
        out_ref[target, 2 * rows :, :span] = high
        out_ref[target, 2 * rows :, span:] = low


def final_kernel(dp_ref, all_ref, key_ref, value_ref, grad_key_ref, grad_value_ref, grad_weight_ref):
    seqs, _, half = all_ref.shape
    channels, span = key_ref.shape
    rows = channels // (2 * seqs)
    lanes = channels // seqs
    for source in range(seqs):
        for turn in range(2):
            owner = dp_ref[0] + turn - 2 * turn * dp_ref[0]
            place = pl.ds(pl.multiple_of(owner * (channels // 2) + source * rows, 8), rows)
            piece = all_ref[source, 2 * turn * rows : 2 * (turn + 1) * rows, :].astype(jnp.float32)
            grad_weight_ref[place, :half] = piece[:rows]
            grad_weight_ref[place, half:] = piece[rows:]
        both = all_ref[source, 4 * rows :, :].astype(jnp.float32)
        mixed = both[:, :span] + both[:, span:]
        place = slice(source * lanes, (source + 1) * lanes)
        grad_key_ref[place, :] = (mixed * value_ref[place, :].astype(jnp.float32)).astype(jnp.bfloat16)
        grad_value_ref[place, :] = (mixed * key_ref[place, :].astype(jnp.float32)).astype(jnp.bfloat16)


def limited(mebibytes):
    return pltpu.CompilerParams(vmem_limit_bytes=mebibytes * 1024 * 1024)


def filter_spectrum(filt, analyse, twist, there):
    channels = filt.shape[0]
    return pl.pallas_call(
        filter_kernel,
        out_shape=jax.ShapeDtypeStruct((channels // 2, 2 * TALL, 2 * WIDE), jnp.float32),
        name="filter_spectrum",
        cost_estimate=pl.CostEstimate(flops=600_000_000, bytes_accessed=2_000_000, transcendentals=0),
    )(filt, analyse, twist, there)


def convolve(signal, spec, tables, conjugate, offset, width):
    analyse, restore, twist, there, back = tables

    def kernel(*refs):
        conv_kernel(conjugate, offset, *refs)

    return pl.pallas_call(
        kernel,
        out_shape=jax.ShapeDtypeStruct(signal.shape[:2] + (width,), jnp.float32),
        name="correlate" if conjugate else "convolve",
        cost_estimate=pl.CostEstimate(flops=4_000_000_000, bytes_accessed=3_000_000, transcendentals=0),
    )(signal, spec, analyse, restore, twist, there, back)


def placed_call(kernel, count, out_shape):
    whole = pl.BlockSpec(memory_space=pltpu.VMEM)
    return pl.pallas_call(
        kernel,
        in_specs=[pl.BlockSpec(memory_space=pltpu.SMEM)] + [whole] * count,
        out_shape=out_shape,
        compiler_params=limited(LIMIT),
        cost_estimate=pl.CostEstimate(flops=600_000_000, bytes_accessed=5_000_000, transcendentals=0),
    )


def gather_features(block, chans):
    def send(values, hop):
        return lax.ppermute(values, "chan", [(k, hop(k)) for k in range(chans)])

    def ahead(k):
        return (k + 2) % chans

    def behind(k):
        return (k - 2) % chans

    half = block.shape[0] // 2
    from_behind = send(block, ahead)
    from_ahead = send(block, behind)
    far_top = send(from_behind[:half], ahead)
    far_bottom = send(from_ahead[half:], behind)
    mine = [block, from_behind, from_ahead, far_top, far_bottom]
    return mine + [send(values, lambda k: k ^ 1) for values in mine]


def swap(blocks, axes="seq"):
    return lax.all_to_all(blocks, axes, split_axis=0, concat_axis=0, tiled=True)


def shards(query_proj, key_proj, value_proj, grad_out, out_weight, long_filter):
    rows, length = long_filter.shape
    seqs, chans, dps = lax.axis_size("seq"), lax.axis_size("chan"), lax.axis_size("dp")
    channels, span = query_proj.shape[1:]
    features = out_weight.shape[1]
    pieces = span // WIDE
    arrived = (np.arange(seqs)[None, :] * pieces + np.arange(pieces)[:, None]).reshape(-1)
    twist, there, back = make_shared()
    analyse_natural, _ = make_tables(np.arange(TALL))
    analyse, restore = make_tables(arrived)
    tables = tuple(jnp.asarray(t) for t in (analyse, restore, twist, there, back))
    place = lax.axis_index("chan").astype(jnp.int32).reshape(1)

    blocks = gather_features(grad_out[0], chans)
    key_vals = key_proj[0].astype(jnp.float32)
    value_vals = value_proj[0].astype(jnp.float32)
    mixed_full = swap((key_vals * value_vals).reshape(seqs, rows, span))
    spec = filter_spectrum(long_filter.reshape(rows, TALL, WIDE), jnp.asarray(analyse_natural), tables[2], tables[3])
    conv_full = convolve(mixed_full, spec, tables, False, 0, span)

    both, grad_mid = placed_call(
        gate_kernel,
        13,
        (
            jax.ShapeDtypeStruct((seqs, rows, 2 * span), jnp.float32),
            jax.ShapeDtypeStruct((channels, span), jnp.float32),
        ),
    )(place, conv_full, query_proj[0], out_weight, *blocks)
    both = swap(both)
    weight_part = placed_call(
        part_kernel, 12, jax.ShapeDtypeStruct((channels, features), jnp.bfloat16)
    )(place, both, query_proj[0], *blocks)
    grad_query = (grad_mid * both[:, :, :span].reshape(channels, span)).astype(jnp.bfloat16)

    group = dps * seqs
    weight_part = swap(weight_part.reshape(group, channels // group, features), ("dp", "seq"))
    back_full = convolve(both, spec, tables, True, span, span)
    scale = 1.0 / math.sqrt(dps * length)
    half = features // 2
    mine = pl.pallas_call(
        lambda *refs: total_kernel(scale, *refs),
        out_shape=jax.ShapeDtypeStruct((2 * (channels // group), half), jnp.bfloat16),
        name="total",
        compiler_params=limited(LIMIT),
    )(weight_part)
    other = lax.ppermute(mine, "dp", [(0, 1), (1, 0)])
    last = pl.pallas_call(
        last_kernel,
        out_shape=jax.ShapeDtypeStruct((seqs, 4 * (channels // group) + rows, half), jnp.bfloat16),
        name="last",
        compiler_params=limited(LIMIT),
    )(mine, other, back_full)
    last = swap(last)
    grad_key, grad_value, grad_weight = placed_call(
        final_kernel,
        3,
        (
            jax.ShapeDtypeStruct((channels, span), jnp.bfloat16),
            jax.ShapeDtypeStruct((channels, span), jnp.bfloat16),
            jax.ShapeDtypeStruct((channels, features), jnp.float32),
        ),
    )(lax.axis_index("dp").astype(jnp.int32).reshape(1), last, key_proj[0], value_proj[0])
    return (grad_query[None], grad_key[None], grad_value[None], grad_weight)


def solution(mesh):
    placed = (
        P("dp", "chan", "seq"),
        P("dp", "chan", "seq"),
        P("dp", "chan", "seq"),
        P("dp", "chan", "seq"),
        P("chan", None),
        P(("chan", "seq"), None),
    )
    return jax.shard_map(
        shards,
        mesh=mesh,
        in_specs=placed,
        out_specs=(
            P("dp", "chan", "seq"),
            P("dp", "chan", "seq"),
            P("dp", "chan", "seq"),
            P("chan", None),
        ),
        check_vma=False,
    )
```

profile of v0, /device:TPU:2, one launch (start us, length us, event | category | flops | bytes accessed | tf_op | source)
XLA Modules:
  0.0 131.3 jit_solution(15994548344909420437)
XLA Ops:
  0.6 0.0 copy-start.2
  0.6 0.0 copy-start.10
  0.7 2.0 %convert_multiply_fusion = f32[1,256,512]{2,1,0:T(8,128)} fusion(bf16[1,256,512]{2,1,0:T(8,128)(2,1)} %param.14, bf16[1,256,512]{2,1,0:T(8,128)(2,1)} %param.13), kind=kLoop, calls=%fused_computation.2 | loop fusion | flops 393216 | bytes 1048576 | tf_op jit(solution)/shard_map/mul | solution.py:290
  2.6 7.5 %all-to-all-start = ((f32[16,16,512]{2,1,0:T(8,128)}), f32[16,16,512]{2,1,0:T(8,128)}, u32[]{:S(2)}, u32[]{:S(2)}) async-start(f32[16,16,512]{2,1,0:T(8,128)} %bitcast.1), calls=%async_computation | async-start | bytes 1048576 | tf_op jit(solution)/shard_map/all_to_all | solution.py:271
  10.1 0.0 copy-done.2
  10.1 6.4 %collective-permute-start.1 = (bf16[256,512]{1,0:T(8,128)(2,1)S(1)}, bf16[256,512]{1,0:T(8,128)(2,1)S(1)}, u32[]{:S(2)}, u32[]{:S(2)}) collective-permute-start(bf16[256,512]{1,0:T(8,128)(2,1)S(1)} %bitcast.20), channel_id=1, source_target_pairs={{0,96},{16,112},{32,0},{48,16},{64,32},{80,48},{96,64},{112,80},{1... | collective-permute-start | bytes 786440 | tf_op jit(solution)/shard_map/ppermute | solution.py:253
  16.5 0.0 collective-permute-start
  16.5 10.7 %collective-permute-done.1.refs_2_ = bf16[256,512]{1,0:T(8,128)(2,1)S(1)} collective-permute-done((bf16[256,512]{1,0:T(8,128)(2,1)S(1)}, bf16[256,512]{1,0:T(8,128)(2,1)S(1)}, u32[]{:S(2)}, u32[]{:S(2)}) %collective-permute-start.1) | collective-permute-done | bytes 262176 | tf_op jit(solution)/shard_map/ppermute | solution.py:253
  27.2 4.7 %collective-permute-start.3 = (bf16[128,512]{1,0:T(8,128)(2,1)S(1)}, bf16[128,512]{1,0:T(8,128)(2,1)S(1)}, u32[]{:S(2)}, u32[]{:S(2)}) collective-permute-start(bf16[128,512]{1,0:T(8,128)(2,1)S(1)} %slice.13), channel_id=1, source_target_pairs={{0,96},{16,112},{32,0},{48,16},{64,32},{80,48},{96,64},{112,80},{1... | collective-permute-start | bytes 393224 | tf_op jit(solution)/shard_map/ppermute | solution.py:253
  31.8 0.0 collective-permute-done.refs_1_
  31.8 0.1 collective-permute-start.2
  31.9 0.1 collective-permute-start.4
  32.0 0.0 copy-done.10
  32.1 0.9 copy.16
  32.9 3.5 %filter_spectrum.1.refs_1_ = f32[8,128,256]{2,1,0:T(8,128)} custom-call(f32[16,64,128]{2,1,0:T(8,128)} %bitcast.28, bf16[128,192]{1,0:T(8,128)(2,1)} %constant.28.clone.analyse_ref, f32[2,64,128]{2,1,0:T(8,128)} %constant.25.clone.twist_ref.refs_4_, bf16[768,256]{1,0:T(8,128)(2,1)} %constant.26.clone.there_ref.refs_5_), custom_call_target="tpu_custom_call" | custom-call | flops 600000000 | bytes 2000000 | tf_op jit(solution)/shard_map/filter_spectrum/pallas_call | solution.py:218
  36.4 0.5 collective-permute-start.6
  36.9 0.1 collective-permute-start.5
  37.0 0.0 collective-permute-done.3.refs_4_
  37.0 0.4 collective-permute-start.8
  37.4 2.9 %collective-permute-done.2.refs_3_ = bf16[128,512]{1,0:T(8,128)(2,1)S(1)} collective-permute-done((bf16[128,512]{1,0:T(8,128)(2,1)S(1)}, bf16[128,512]{1,0:T(8,128)(2,1)S(1)}, u32[]{:S(2)}, u32[]{:S(2)}) %collective-permute-start.2) | collective-permute-done | bytes 131104 | tf_op jit(solution)/shard_map/ppermute | solution.py:253
  40.3 0.0 collective-permute-start.7
  40.3 0.0 all-to-all-done.refs_0_
  40.3 6.4 %convolve.1.conv_ref = f32[16,16,512]{2,1,0:T(8,128)} custom-call(f32[16,16,512]{2,1,0:T(8,128)} %all-to-all-done.refs_0_, f32[8,128,256]{2,1,0:T(8,128)} %filter_spectrum.1.refs_1_, bf16[128,192]{1,0:T(8,128)(2,1)} %constant.23.clone.refs_2_, bf16[64,384]{1,0:T(8,128)(2,1)} %constant.24.clone.refs_3_, f32[2,64,128]{2,1,0:T(8,128)} %constant.25.clone.twist_ref.refs_4_, ...), custom_call_target="tpu_custom_call" | custom-call | flops 4000000000 | bytes 3000000 | tf_op jit(solution)/shard_map/convolve/pallas_call | solution.py:232
  46.7 0.0 collective-permute-done.4.refs_5_
  46.7 0.0 collective-permute-done.8.refs_9_
  46.7 0.0 collective-permute-done.6.refs_7_
  46.7 0.0 collective-permute-done.7.refs_8_
  46.7 0.0 collective-permute-done.5.refs_6_
  46.7 0.0 copy-done.1
  46.7 1.0 copy-done.4
  47.8 0.9 shard_map.147
  48.6 0.0 copy-start.5
  48.6 23.5 %all_to_all.20.both_ref.refs_0_ = f32[16,16,1024]{2,1,0:T(8,128)S(1)} all-to-all(f32[16,16,1024]{2,1,0:T(8,128)S(1)} %get-tuple-element.10), channel_id=1, replica_groups=mesh['dp'=2,'chan'=8,'seq'=16] {'seq'}, dimensions={0} | all-to-all | bytes 2097152 | tf_op jit(solution)/shard_map/all_to_all | solution.py:271
  72.2 0.9 shard_map.148
  73.1 0.1 copy-done
  73.2 19.7 %all_to_all.21.refs_0_ = bf16[32,8,2048]{2,1,0:T(8,128)(2,1)S(1)} all-to-all(bf16[32,8,2048]{2,1,0:T(8,128)(2,1)S(1)} %bitcast.17), channel_id=1, replica_groups=mesh['dp'=2,'chan'=8,'seq'=16] {'dp','seq'}, dimensions={0} | all-to-all | bytes 2097152 | tf_op jit(solution)/shard_map/all_to_all | solution.py:271
  92.9 0.2 total.1.mine_ref
  93.1 1.5 %collective-permute-start.9 = (bf16[16,1024]{1,0:T(8,128)(2,1)S(1)}, bf16[16,1024]{1,0:T(8,128)(2,1)S(1)}, u32[]{:S(2)}, u32[]{:S(2)}) collective-permute-start(bf16[16,1024]{1,0:T(8,128)(2,1)S(1)} %total.1.mine_ref), channel_id=1, source_target_pairs={{0,128},{128,0},{1,129},{129,1},{2,130},{130,2},{3,131},{131,3},{4... | collective-permute-start | bytes 98312 | tf_op jit(solution)/shard_map/ppermute | solution.py:319
  94.5 6.5 %correlate.1.back_ref = f32[16,16,512]{2,1,0:T(8,128)} custom-call(f32[16,16,1024]{2,1,0:T(8,128)} %copy-done, f32[8,128,256]{2,1,0:T(8,128)} %filter_spectrum.1.refs_1_, bf16[128,192]{1,0:T(8,128)(2,1)} %constant.23.clone.refs_2_, bf16[64,384]{1,0:T(8,128)(2,1)} %constant.24.clone.refs_3_, f32[2,64,128]{2,1,0:T(8,128)} %constant.25.clone.twist_ref.refs_4_, ...), custom_call_target="tpu_custom_call" | custom-call | flops 4000000000 | bytes 3000000 | tf_op jit(solution)/shard_map/correlate/pallas_call | solution.py:232
  101.0 0.0 collective-permute-done.9.other_ref
  101.1 1.0 copy-done.7
  102.1 1.3 last.1
  103.4 5.4 %all-to-all-start.3 = ((bf16[16,48,1024]{2,1,0:T(8,128)(2,1)}), bf16[16,48,1024]{2,1,0:T(8,128)(2,1)S(1)}, u32[]{:S(2)}, u32[]{:S(2)}) async-start(bf16[16,48,1024]{2,1,0:T(8,128)(2,1)} %last.1), calls=%async_computation.3 | async-start | bytes 3145728 | tf_op jit(solution)/shard_map/all_to_all | solution.py:271
  108.8 0.0 copy-start.9
  108.8 0.8 fusion
  109.6 20.0 %all-to-all-done.3.all_ref = bf16[16,48,1024]{2,1,0:T(8,128)(2,1)S(1)} async-done(((bf16[16,48,1024]{2,1,0:T(8,128)(2,1)}), bf16[16,48,1024]{2,1,0:T(8,128)(2,1)S(1)}, u32[]{:S(2)}, u32[]{:S(2)}) %all-to-all-start.3) | async-done | bytes 1572896 | tf_op jit(solution)/shard_map/all_to_all | solution.py:271
  129.6 0.0 copy-done.9
  129.6 1.7 %shard_map.149 = (bf16[256,512]{1,0:T(8,128)(2,1)}, bf16[256,512]{1,0:T(8,128)(2,1)}, f32[256,2048]{1,0:T(8,128)}) custom-call(s32[1]{0:T(128)} %bitcast.6.dp_ref, bf16[16,48,1024]{2,1,0:T(8,128)(2,1)S(1)} %all-to-all-done.3.all_ref, bf16[256,512]{1,0:T(8,128)(2,1)S(1)} %bitcast.26, bf16[256,512]{1,0:T(8,128)(2,1)S(1)} %bitcast.25), custom_call_target="tpu_custom_call" | custom-call | flops 600000000 | bytes 5000000 | tf_op jit(solution)/shard_map/pallas_call | solution.py:327
  (15 shorter events, 0.0 us)
Async XLA Ops:
  0.6 9.5 %copy-start.2 = (bf16[1,256,512]{2,1,0:T(8,128)(2,1)S(1)}, bf16[1,256,512]{2,1,0:T(8,128)(2,1)}, u32[]{:S(2)}) copy-start(bf16[1,256,512]{2,1,0:T(8,128)(2,1)} %param.15) | copy-start | bytes 786436
  0.6 31.4 %copy-start.10 = (f32[16,8192]{1,0:T(8,128)S(1)}, f32[16,8192]{1,0:T(8,128)}, u32[]{:S(2)}) copy-start(f32[16,8192]{1,0:T(8,128)} %param.17) | copy-start | bytes 1572868
  2.6 37.6 %all-to-all-start = ((f32[16,16,512]{2,1,0:T(8,128)}), f32[16,16,512]{2,1,0:T(8,128)}, u32[]{:S(2)}, u32[]{:S(2)}) async-start(f32[16,16,512]{2,1,0:T(8,128)} %bitcast.1), calls=%async_computation | async-start | bytes 1048576 | tf_op jit(solution)/shard_map/all_to_all | solution.py:271
  10.1 17.0 %collective-permute-start.1 = (bf16[256,512]{1,0:T(8,128)(2,1)S(1)}, bf16[256,512]{1,0:T(8,128)(2,1)S(1)}, u32[]{:S(2)}, u32[]{:S(2)}) collective-permute-start(bf16[256,512]{1,0:T(8,128)(2,1)S(1)} %bitcast.20), channel_id=1, source_target_pairs={{0,96},{16,112},{32,0},{48,16},{64,32},{80,48},{96,64},{112,80},{1... | collective-permute-start | bytes 786440 | tf_op jit(solution)/shard_map/ppermute | solution.py:253
  16.5 15.3 %collective-permute-start = (bf16[256,512]{1,0:T(8,128)(2,1)S(1)}, bf16[256,512]{1,0:T(8,128)(2,1)S(1)}, u32[]{:S(2)}, u32[]{:S(2)}) collective-permute-start(bf16[256,512]{1,0:T(8,128)(2,1)S(1)} %bitcast.21), channel_id=1, source_target_pairs={{0,32},{16,48},{32,64},{48,80},{64,96},{80,112},{96,0},{112,16},{1... | collective-permute-start | bytes 786440 | tf_op jit(solution)/shard_map/ppermute | solution.py:253
  27.2 9.8 %collective-permute-start.3 = (bf16[128,512]{1,0:T(8,128)(2,1)S(1)}, bf16[128,512]{1,0:T(8,128)(2,1)S(1)}, u32[]{:S(2)}, u32[]{:S(2)}) collective-permute-start(bf16[128,512]{1,0:T(8,128)(2,1)S(1)} %slice.13), channel_id=1, source_target_pairs={{0,96},{16,112},{32,0},{48,16},{64,32},{80,48},{96,64},{112,80},{1... | collective-permute-start | bytes 393224 | tf_op jit(solution)/shard_map/ppermute | solution.py:253
  31.8 8.4 %collective-permute-start.2 = (bf16[128,512]{1,0:T(8,128)(2,1)S(1)}, bf16[128,512]{1,0:T(8,128)(2,1)S(1)}, u32[]{:S(2)}, u32[]{:S(2)}) collective-permute-start(bf16[128,512]{1,0:T(8,128)(2,1)S(1)} %slice.12), channel_id=1, source_target_pairs={{0,32},{16,48},{32,64},{48,80},{64,96},{80,112},{96,0},{112,16},{1... | collective-permute-start | bytes 393224 | tf_op jit(solution)/shard_map/ppermute | solution.py:253
  31.9 14.7 %collective-permute-start.4 = (bf16[256,512]{1,0:T(8,128)(2,1)S(1)}, bf16[256,512]{1,0:T(8,128)(2,1)S(1)}, u32[]{:S(2)}, u32[]{:S(2)}) collective-permute-start(bf16[256,512]{1,0:T(8,128)(2,1)S(1)} %bitcast.22), channel_id=1, source_target_pairs={{0,16},{16,0},{32,48},{48,32},{64,80},{80,64},{96,112},{112,96},{1... | collective-permute-start | bytes 786440 | tf_op jit(solution)/shard_map/ppermute | solution.py:253
  36.4 10.3 %copy-start.1 = (bf16[1,256,512]{2,1,0:T(8,128)(2,1)S(1)}, bf16[1,256,512]{2,1,0:T(8,128)(2,1)}, u32[]{:S(2)}) copy-start(bf16[1,256,512]{2,1,0:T(8,128)(2,1)} %param.12) | copy-start | bytes 786436
  36.4 10.3 %copy-start.3 = (bf16[256,2048]{1,0:T(8,128)(2,1)S(1)}, bf16[256,2048]{1,0:T(8,128)(2,1)}, u32[]{:S(2)}) copy-start(bf16[256,2048]{1,0:T(8,128)(2,1)} %weight_ref.1) | copy-start | bytes 3145732
  36.4 10.3 %collective-permute-start.6 = (bf16[256,512]{1,0:T(8,128)(2,1)S(1)}, bf16[256,512]{1,0:T(8,128)(2,1)S(1)}, u32[]{:S(2)}, u32[]{:S(2)}) collective-permute-start(bf16[256,512]{1,0:T(8,128)(2,1)S(1)} %collective-permute-done.1.refs_2_), channel_id=1, source_target_pairs={{0,16},{16,0},{32,48},{48,32},{64,80},{80,64},{96,112},{112,96},{1... | collective-permute-start | bytes 786440 | tf_op jit(solution)/shard_map/ppermute | solution.py:253
  36.9 9.8 %collective-permute-start.5 = (bf16[256,512]{1,0:T(8,128)(2,1)S(1)}, bf16[256,512]{1,0:T(8,128)(2,1)S(1)}, u32[]{:S(2)}, u32[]{:S(2)}) collective-permute-start(bf16[256,512]{1,0:T(8,128)(2,1)S(1)} %collective-permute-done.refs_1_), channel_id=1, source_target_pairs={{0,16},{16,0},{32,48},{48,32},{64,80},{80,64},{96,112},{112,96},{1... | collective-permute-start | bytes 786440 | tf_op jit(solution)/shard_map/ppermute | solution.py:253
  37.0 9.7 %collective-permute-start.8 = (bf16[128,512]{1,0:T(8,128)(2,1)S(1)}, bf16[128,512]{1,0:T(8,128)(2,1)S(1)}, u32[]{:S(2)}, u32[]{:S(2)}) collective-permute-start(bf16[128,512]{1,0:T(8,128)(2,1)S(1)} %collective-permute-done.3.refs_4_), channel_id=1, source_target_pairs={{0,16},{16,0},{32,48},{48,32},{64,80},{80,64},{96,112},{112,96},{1... | collective-permute-start | bytes 393224 | tf_op jit(solution)/shard_map/ppermute | solution.py:253
  40.3 6.4 %collective-permute-start.7 = (bf16[128,512]{1,0:T(8,128)(2,1)S(1)}, bf16[128,512]{1,0:T(8,128)(2,1)S(1)}, u32[]{:S(2)}, u32[]{:S(2)}) collective-permute-start(bf16[128,512]{1,0:T(8,128)(2,1)S(1)} %collective-permute-done.2.refs_3_), channel_id=1, source_target_pairs={{0,16},{16,0},{32,48},{48,32},{64,80},{80,64},{96,112},{112,96},{1... | collective-permute-start | bytes 393224 | tf_op jit(solution)/shard_map/ppermute | solution.py:253
  46.7 1.0 copy-start.4
  48.6 24.5 %copy-start.5 = (f32[256,512]{1,0:T(8,128)}, f32[256,512]{1,0:T(8,128)S(1)}, u32[]{:S(2)}) copy-start(f32[256,512]{1,0:T(8,128)S(1)} %get-tuple-element.9) | copy-start | bytes 1572868
  72.2 1.0 copy-start
  93.1 8.0 %collective-permute-start.9 = (bf16[16,1024]{1,0:T(8,128)(2,1)S(1)}, bf16[16,1024]{1,0:T(8,128)(2,1)S(1)}, u32[]{:S(2)}, u32[]{:S(2)}) collective-permute-start(bf16[16,1024]{1,0:T(8,128)(2,1)S(1)} %total.1.mine_ref), channel_id=1, source_target_pairs={{0,128},{128,0},{1,129},{129,1},{2,130},{130,2},{3,131},{131,3},{4... | collective-permute-start | bytes 98312 | tf_op jit(solution)/shard_map/ppermute | solution.py:319
  101.0 1.0 copy-start.7
  103.4 5.4 %slice-start = ((f32[16,16,1024]{2,1,0:T(8,128)}), f32[16,16,512]{2,1,0:T(8,128)S(1)}, s32[]{:S(2)}) async-start(f32[16,16,1024]{2,1,0:T(8,128)} %copy-done), calls=%async_computation.4 | async-start | bytes 1048576 | tf_op jit(solution)/shard_map/slice | solution.py:306
  103.4 5.4 %copy-start.6 = (f32[256,512]{1,0:T(8,128)S(1)}, f32[256,512]{1,0:T(8,128)}, u32[]{:S(2)}) copy-start(f32[256,512]{1,0:T(8,128)} %copy-done.5) | copy-start | bytes 1572868
  103.4 26.3 %all-to-all-start.3 = ((bf16[16,48,1024]{2,1,0:T(8,128)(2,1)}), bf16[16,48,1024]{2,1,0:T(8,128)(2,1)S(1)}, u32[]{:S(2)}, u32[]{:S(2)}) async-start(bf16[16,48,1024]{2,1,0:T(8,128)(2,1)} %last.1), calls=%async_computation.3 | async-start | bytes 3145728 | tf_op jit(solution)/shard_map/all_to_all | solution.py:271
  108.8 20.9 %copy-start.8 = (bf16[1,256,512]{2,1,0:T(8,128)(2,1)S(1)}, bf16[1,256,512]{2,1,0:T(8,128)(2,1)}, u32[]{:S(2)}) copy-start(bf16[1,256,512]{2,1,0:T(8,128)(2,1)} %param.14) | copy-start | bytes 786436
  108.8 20.9 %copy-start.9 = (bf16[1,256,512]{2,1,0:T(8,128)(2,1)S(1)}, bf16[1,256,512]{2,1,0:T(8,128)(2,1)}, u32[]{:S(2)}) copy-start(bf16[1,256,512]{2,1,0:T(8,128)(2,1)} %param.13) | copy-start | bytes 786436
where the time goes:
time: 132 us; the launch traced here: 131 us
  blocking collectives  43.3 us (33%)
  waiting for transfers between devices  33.6 us (25%)
  starting transfers between devices  26.5 us (20%)
  Pallas kernels  21.2 us (16%)
  local copies, waits for them, and re-layouts  3.09 us (2%)
  other arithmetic  2.79 us (2%)
    all_to_all x2, blocking collectives, swap(): return lax.all_to_all(blocks, axes, split_axis=0, concat_axis=0, tiled=True)  43.3 us
    all_to_all x2, waiting for transfers between devices, swap(): return lax.all_to_all(blocks, axes, split_axis=0, concat_axis=0, tiled=True)  20 us
    ppermute x9, waiting for transfers between devices, send(): return lax.ppermute(values, 'chan', [(k, hop(k)) for k in range(chans)])  13.5 us
    all_to_all x2, starting transfers between devices, swap(): return lax.all_to_all(blocks, axes, split_axis=0, concat_axis=0, tiled=True)  12.9 us
    pallas_call x2, Pallas kernels, convolve(): pl.pallas_call(kernel, out_shape=jax.ShapeDtypeStruct(signal.shape[:2] +...  12.9 us
    ppermute x9, starting transfers between devices, send(): return lax.ppermute(values, 'chan', [(k, hop(k)) for k in range(chans)])  12.2 us
    pallas_call x1, Pallas kernels, filter_spectrum(): pl.pallas_call(filter_kernel, out_shape=jax.ShapeDtypeStruct((channels //...  3.46 us
    unnamed x23, local copies, waits for them, and re-layouts  3.07 us
  transfers between devices with their start and end apart: 12, of which 3 were waited for; matrix products, arithmetic and copies ran while one was open for 1% of the time, Pallas kernels for 12%

commit v1 on v0

--- a/solution.py
+++ b/solution.py
@@ -13,6 +13,7 @@
 WIDE = 128
 TALL = 64
 LIMIT = 20
+BATCH = 8
 
 
 def split_table(values):
@@ -70,60 +71,80 @@
     return jnp.concatenate([high, low, high], axis=1)
 
 
-def forward_pair(pair, analyse, twist, there):
-    both = dot(analyse, stacked(jnp.concatenate(pair, axis=1)))
+def forward_group(inputs, analyse, twist, there):
+    both = dot(analyse, stacked(jnp.concatenate(inputs, axis=1)))
     cos, sin = twist[0], twist[1]
     rows = []
-    for which in range(2):
+    for which in range(len(inputs)):
         real = both[:TALL, which * WIDE : (which + 1) * WIDE]
         imag = both[TALL:, which * WIDE : (which + 1) * WIDE]
         rows.append(jnp.concatenate([real * cos + imag * sin, imag * cos - real * sin], axis=1))
     return dot(beside(jnp.concatenate(rows, axis=0)), there)
 
 
-def inverse_pair(spec, restore, twist, back):
+def inverse_group(spec, restore, twist, back):
     both = dot(beside(spec), back)
     cos, sin = twist[0], twist[1]
     columns = []
-    for which in range(2):
+    for which in range(spec.shape[0] // TALL):
         real = both[which * TALL : (which + 1) * TALL, :WIDE]
         imag = both[which * TALL : (which + 1) * TALL, WIDE:]
         columns.append(jnp.concatenate([real * cos - imag * sin, real * sin + imag * cos], axis=0))
     return dot(restore, stacked(jnp.concatenate(columns, axis=1)))
 
 
-def filter_kernel(filt_ref, analyse_ref, twist_ref, there_ref, spec_ref):
-    twist = twist_ref[...]
-    for pair in range(filt_ref.shape[0] // 2):
-        inputs = [filt_ref[2 * pair], filt_ref[2 * pair + 1]]
-        spec_ref[pair] = forward_pair(inputs, analyse_ref[...], twist, there_ref[...])
-
-
-def conv_kernel(conjugate, offset, signal_ref, spec_ref, analyse_ref, restore_ref, twist_ref, there_ref, back_ref, out_ref):
+def product(left, right, conjugate):
+    real, imag = left[:, :WIDE], left[:, WIDE:]
+    other_real, other_imag = right[:, :WIDE], right[:, WIDE:]
+    if conjugate:
+        other_imag = -other_imag
+    return jnp.concatenate(
+        [real * other_real - imag * other_imag, real * other_imag + imag * other_real], axis=1
+    )
+
+
+def arrived_rows(signal_ref, channel, offset, width):
+    rows = signal_ref[:, channel, offset : offset + width]
+    return jnp.concatenate([rows[:, q * WIDE : (q + 1) * WIDE] for q in range(width // WIDE)], axis=0)
+
+
+def sent_rows(result, which, blocks):
+    column = result[:, which * WIDE : (which + 1) * WIDE]
+    return jnp.concatenate(
+        [column[q * blocks : (q + 1) * blocks] for q in range(TALL // blocks)], axis=1
+    )
+
+
+def convolve_kernel(signal_ref, filt_ref, natural_ref, analyse_ref, restore_ref, twist_ref, there_ref, back_ref, out_ref, spec_ref, rows_ref):
     twist = twist_ref[...]
     blocks, channels, width = out_ref.shape
-    pieces = width // WIDE
-    for pair in range(channels // 2):
-        inputs = []
-        for channel in (2 * pair, 2 * pair + 1):
-            rows = signal_ref[:, channel, offset : offset + width]
-            inputs.append(
-                jnp.concatenate([rows[:, q * WIDE : (q + 1) * WIDE] for q in range(pieces)], axis=0)
-            )
-        spec = forward_pair(inputs, analyse_ref[...], twist, there_ref[...])
-        real, imag = spec[:, :WIDE], spec[:, WIDE:]
-        filt = spec_ref[pair]
-        filt_real, filt_imag = filt[:, :WIDE], filt[:, WIDE:]
-        if conjugate:
-            filt_imag = -filt_imag
-        product = jnp.concatenate(
-            [real * filt_real - imag * filt_imag, real * filt_imag + imag * filt_real], axis=1
-        )
-        result = inverse_pair(product, restore_ref[...], twist, back_ref[...])
-        for which in range(2):
-            column = result[:, which * WIDE : (which + 1) * WIDE]
-            row = jnp.concatenate([column[q * blocks : (q + 1) * blocks] for q in range(pieces)], axis=1)
-            out_ref[:, 2 * pair + which, :] = row
+    for place in range(TALL):
+        rows_ref[place] = filt_ref[:, place * WIDE : (place + 1) * WIDE]
+    for group in range(channels // BATCH):
+        members = range(group * BATCH, (group + 1) * BATCH)
+        filt = forward_group([rows_ref[:, m, :] for m in members], natural_ref[...], twist, there_ref[...])
+        spec_ref[group] = filt
+        inputs = [arrived_rows(signal_ref, m, 0, width) for m in members]
+        spec = forward_group(inputs, analyse_ref[...], twist, there_ref[...])
+        result = inverse_group(product(spec, filt, False), restore_ref[...], twist, back_ref[...])
+        for which, m in enumerate(members):
+            out_ref[:, m, :] = sent_rows(result, which, blocks)
+
+
+def correlate_kernel(signal_ref, spec_ref, analyse_ref, restore_ref, twist_ref, there_ref, back_ref, out_ref, rows_ref):
+    twist = twist_ref[...]
+    blocks, channels, width = rows_ref.shape
+    below = out_ref.shape[1] - channels
+    for group in range(channels // BATCH):
+        members = range(group * BATCH, (group + 1) * BATCH)
+        inputs = [arrived_rows(signal_ref, m, width, width) for m in members]
+        spec = forward_group(inputs, analyse_ref[...], twist, there_ref[...])
+        result = inverse_group(product(spec, spec_ref[group], True), restore_ref[...], twist, back_ref[...])
+        for which, m in enumerate(members):
+            rows_ref[:, m, :] = sent_rows(result, which, blocks)
+    high, low = halves(rows_ref[...])
+    out_ref[:, below:, :width] = high
+    out_ref[:, below:, width:] = low
 
 
 def places(place_ref, step):
@@ -140,19 +161,26 @@
     return out
 
 
+def mix_kernel(key_ref, value_ref, out_ref):
+    mixed = key_ref[...].astype(jnp.float32) * value_ref[...].astype(jnp.float32)
+    out_ref[...] = mixed.reshape(out_ref.shape)
+
+
 def gate_kernel(place_ref, conv_ref, query_ref, weight_ref, *refs):
-    blocks, (both_ref, mid_ref) = refs[:10], refs[10:]
+    blocks, (both_ref, mid_ref, sem) = refs[:10], refs[10:]
     step = blocks[0].shape[0]
+    seqs, rows, width = conv_ref.shape
+    copy = pltpu.make_async_copy(conv_ref, both_ref.at[:, :, :width], sem)
+    copy.start()
     total = None
     for (start, size), block in zip(places(place_ref, step), blocks):
         columns = weight_ref[:, pl.ds(pl.multiple_of(start, WIDE), size)]
         term = dot(columns, block[...])
         total = term if total is None else total + term
     mid_ref[...] = total
-    seqs, rows, width = conv_ref.shape
-    both_ref[:, :, :width] = conv_ref[...]
     gate = query_ref[...].astype(jnp.float32) * total
     both_ref[:, :, width:] = gate.reshape(seqs, rows, width)
+    copy.wait()
 
 
 def part_kernel(place_ref, both_ref, query_ref, *refs):
@@ -179,15 +207,17 @@
     out_ref[rows:, :] = total[:, half:]
 
 
-def last_kernel(mine_ref, other_ref, back_ref, out_ref):
-    seqs, _, span = back_ref.shape
+def last_kernel(mine_ref, other_ref, back_ref, out_ref, sems):
     rows = mine_ref.shape[0]
-    for target in range(seqs):
-        out_ref[target, :rows, :] = mine_ref[...]
-        out_ref[target, rows : 2 * rows, :] = other_ref[...]
-        high, low = halves(back_ref[target])
-        out_ref[target, 2 * rows :, :span] = high
-        out_ref[target, 2 * rows :, span:] = low
+    copies = []
+    for target in range(out_ref.shape[0]):
+        for turn, source in enumerate((mine_ref, other_ref)):
+            place = out_ref.at[target, turn * rows : (turn + 1) * rows, :]
+            copies.append(pltpu.make_async_copy(source, place, sems.at[target, turn]))
+    for copy in copies:
+        copy.start()
+    for copy in copies:
+        copy.wait()
 
 
 def final_kernel(dp_ref, all_ref, key_ref, value_ref, grad_key_ref, grad_value_ref, grad_weight_ref):
@@ -213,35 +243,39 @@
     return pltpu.CompilerParams(vmem_limit_bytes=mebibytes * 1024 * 1024)
 
 
-def filter_spectrum(filt, analyse, twist, there):
-    channels = filt.shape[0]
+def convolve(signal, filt, natural, tables):
+    _, channels, _ = signal.shape
     return pl.pallas_call(
-        filter_kernel,
-        out_shape=jax.ShapeDtypeStruct((channels // 2, 2 * TALL, 2 * WIDE), jnp.float32),
-        name="filter_spectrum",
-        cost_estimate=pl.CostEstimate(flops=600_000_000, bytes_accessed=2_000_000, transcendentals=0),
-    )(filt, analyse, twist, there)
-
-
-def convolve(signal, spec, tables, conjugate, offset, width):
-    analyse, restore, twist, there, back = tables
-
-    def kernel(*refs):
-        conv_kernel(conjugate, offset, *refs)
-
+        convolve_kernel,
+        out_shape=(
+            jax.ShapeDtypeStruct(signal.shape, jnp.float32),
+            jax.ShapeDtypeStruct((channels // BATCH, BATCH * TALL, 2 * WIDE), jnp.float32),
+        ),
+        scratch_shapes=[pltpu.VMEM((TALL, channels, WIDE), jnp.float32)],
+        name="convolve",
+        cost_estimate=pl.CostEstimate(flops=4_000_000_000, bytes_accessed=3_000_000, transcendentals=0),
+    )(signal, filt, natural, *tables)
+
+
+def correlate(both, spec, tables, above):
+    blocks, channels, double = both.shape
     return pl.pallas_call(
-        kernel,
-        out_shape=jax.ShapeDtypeStruct(signal.shape[:2] + (width,), jnp.float32),
-        name="correlate" if conjugate else "convolve",
+        correlate_kernel,
+        out_shape=jax.ShapeDtypeStruct((blocks, above + channels, double), jnp.bfloat16),
+        scratch_shapes=[pltpu.VMEM((blocks, channels, double // 2), jnp.float32)],
+        name="correlate",
         cost_estimate=pl.CostEstimate(flops=4_000_000_000, bytes_accessed=3_000_000, transcendentals=0),
-    )(signal, spec, analyse, restore, twist, there, back)
-
-
-def placed_call(kernel, count, out_shape):
+    )(both, spec, *tables)
+
+
+def placed_call(kernel, count, out_shape, left=()):
     whole = pl.BlockSpec(memory_space=pltpu.VMEM)
     return pl.pallas_call(
         kernel,
-        in_specs=[pl.BlockSpec(memory_space=pltpu.SMEM)] + [whole] * count,
+        in_specs=[pl.BlockSpec(memory_space=pltpu.SMEM)]
+        + [pl.BlockSpec(memory_space=pltpu.HBM)] * len(left)
+        + [whole] * (count - len(left)),
+        scratch_shapes=[pltpu.SemaphoreType.DMA] * len(left),
         out_shape=out_shape,
         compiler_params=limited(LIMIT),
         cost_estimate=pl.CostEstimate(flops=600_000_000, bytes_accessed=5_000_000, transcendentals=0),
@@ -285,11 +319,13 @@
     place = lax.axis_index("chan").astype(jnp.int32).reshape(1)
 
     blocks = gather_features(grad_out[0], chans)
-    key_vals = key_proj[0].astype(jnp.float32)
-    value_vals = value_proj[0].astype(jnp.float32)
-    mixed_full = swap((key_vals * value_vals).reshape(seqs, rows, span))
-    spec = filter_spectrum(long_filter.reshape(rows, TALL, WIDE), jnp.asarray(analyse_natural), tables[2], tables[3])
-    conv_full = convolve(mixed_full, spec, tables, False, 0, span)
+    mixed_in = pl.pallas_call(
+        mix_kernel,
+        out_shape=jax.ShapeDtypeStruct((seqs, rows, span), jnp.float32),
+        name="mix",
+    )(key_proj[0], value_proj[0])
+    mixed_full = swap(mixed_in)
+    conv_full, spec = convolve(mixed_full, long_filter, jnp.asarray(analyse_natural), tables)
 
     both, grad_mid = placed_call(
         gate_kernel,
@@ -298,7 +334,8 @@
             jax.ShapeDtypeStruct((seqs, rows, 2 * span), jnp.float32),
             jax.ShapeDtypeStruct((channels, span), jnp.float32),
         ),
-    )(place, conv_full, query_proj[0], out_weight, *blocks)
+        left=(0,),
+    )(place, pltpu.with_memory_space_constraint(conv_full, pltpu.HBM), query_proj[0], out_weight, *blocks)
     both = swap(both)
     weight_part = placed_call(
         part_kernel, 12, jax.ShapeDtypeStruct((channels, features), jnp.bfloat16)
@@ -307,7 +344,7 @@
 
     group = dps * seqs
     weight_part = swap(weight_part.reshape(group, channels // group, features), ("dp", "seq"))
-    back_full = convolve(both, spec, tables, True, span, span)
+    back_full = correlate(both, spec, tables, 4 * (channels // group))
     scale = 1.0 / math.sqrt(dps * length)
     half = features // 2
     mine = pl.pallas_call(
@@ -317,12 +354,18 @@
         compiler_params=limited(LIMIT),
     )(weight_part)
     other = lax.ppermute(mine, "dp", [(0, 1), (1, 0)])
+    whole = pl.BlockSpec(memory_space=pltpu.VMEM)
+    left = pl.BlockSpec(memory_space=pltpu.HBM)
     last = pl.pallas_call(
         last_kernel,
-        out_shape=jax.ShapeDtypeStruct((seqs, 4 * (channels // group) + rows, half), jnp.bfloat16),
+        in_specs=[whole, whole, left],
+        out_specs=left,
+        out_shape=jax.ShapeDtypeStruct(back_full.shape, back_full.dtype),
+        input_output_aliases={2: 0},
+        scratch_shapes=[pltpu.SemaphoreType.DMA((seqs, 2))],
         name="last",
         compiler_params=limited(LIMIT),
-    )(mine, other, back_full)
+    )(mine, other, pltpu.with_memory_space_constraint(back_full, pltpu.HBM))
     last = swap(last)
     grad_key, grad_value, grad_weight = placed_call(
         final_kernel,

time: 132 us -> 129 us (0.977)
  waiting for transfers between devices: 33.6 us -> 38.3 us
  local copies, waits for them, and re-layouts: 3.09 us -> 0.08 us
  Pallas kernels: 21.2 us -> 18.4 us
  other arithmetic: 2.79 us -> 0.8 us
    ppermute x9, waiting for transfers between devices: 13.5 us -> 18.3 us  [send(): return lax.ppermute(values, 'chan', [(k, hop(k)) for k in range(chans)])]
    pallas_call x4, Pallas kernels: 17.6 us -> 13.9 us  [the longest x1 5.46 us: correlate(): pl.pallas_call(correlate_kernel, out_shape=jax.ShapeDtypeStruct((blocks,...]
    unnamed x23 -> x16, local copies, waits for them, and re-layouts: 3.07 us -> 0.06 us
    mul x1 -> x0, other arithmetic: 1.99 us -> none  [shards(): mixed_full = swap((key_vals * value_vals).reshape(seqs, rows, span))]
  transfers between devices with their start and end apart: 12 -> 12, of which waited for: 3 -> 4; matrix products, arithmetic and copies ran while one was open for 1% -> 1% of each run, Pallas kernels for 12% -> 8%
where the time goes in v1:
time: 129 us; the launch traced here: 128 us
  blocking collectives  43.3 us (34%)
  waiting for transfers between devices  38.3 us (30%)
  starting transfers between devices  26.2 us (20%)
  Pallas kernels  18.4 us (14%)
    all_to_all x2, blocking collectives, swap(): return lax.all_to_all(blocks, axes, split_axis=0, concat_axis=0, tiled=True)  43.3 us
    all_to_all x2, waiting for transfers between devices, swap(): return lax.all_to_all(blocks, axes, split_axis=0, concat_axis=0, tiled=True)  20 us
    ppermute x9, waiting for transfers between devices, send(): return lax.ppermute(values, 'chan', [(k, hop(k)) for k in range(chans)])  18.3 us
    all_to_all x2, starting transfers between devices, swap(): return lax.all_to_all(blocks, axes, split_axis=0, concat_axis=0, tiled=True)  12.9 us
    ppermute x9, starting transfers between devices, send(): return lax.ppermute(values, 'chan', [(k, hop(k)) for k in range(chans)])  11.8 us
    pallas_call x1, Pallas kernels, correlate(): pl.pallas_call(correlate_kernel, out_shape=jax.ShapeDtypeStruct((blocks,...  5.46 us
    pallas_call x1, Pallas kernels, convolve(): pl.pallas_call(convolve_kernel, out_shape=(jax.ShapeDtypeStruct(signal.sh...  5.32 us
  transfers between devices with their start and end apart: 12, of which 4 were waited for; matrix products, arithmetic and copies ran while one was open for 1% of the time, Pallas kernels for 8%

profile of v1, /device:TPU:2, one launch (start us, length us, event | category | flops | bytes accessed | tf_op | source)
XLA Modules:
  0.0 127.8 jit_solution(13986326724154272253)
XLA Ops:
  0.6 0.0 copy-start.2
  0.6 1.9 %mix.1 = f32[16,16,512]{2,1,0:T(8,128)} custom-call(bf16[256,512]{1,0:T(8,128)(2,1)} %bitcast.22, bf16[256,512]{1,0:T(8,128)(2,1)} %bitcast.24), custom_call_target="tpu_custom_call" | custom-call | tf_op jit(solution)/shard_map/mix/pallas_call | solution.py:322
  2.6 7.5 %all-to-all-start = ((f32[16,16,512]{2,1,0:T(8,128)}), f32[16,16,512]{2,1,0:T(8,128)}, u32[]{:S(2)}, u32[]{:S(2)}) async-start(f32[16,16,512]{2,1,0:T(8,128)} %mix.1), calls=%async_computation | async-start | bytes 1048576 | tf_op jit(solution)/shard_map/all_to_all | solution.py:305
  10.0 0.0 copy-done.2
  10.0 6.4 %collective-permute-start.1 = (bf16[256,512]{1,0:T(8,128)(2,1)S(1)}, bf16[256,512]{1,0:T(8,128)(2,1)S(1)}, u32[]{:S(2)}, u32[]{:S(2)}) collective-permute-start(bf16[256,512]{1,0:T(8,128)(2,1)S(1)} %bitcast.17), channel_id=1, source_target_pairs={{0,96},{16,112},{32,0},{48,16},{64,32},{80,48},{96,64},{112,80},{1... | collective-permute-start | bytes 786440 | tf_op jit(solution)/shard_map/ppermute | solution.py:287
  16.4 0.0 collective-permute-start
  16.4 10.7 %collective-permute-done.1.refs_2_ = bf16[256,512]{1,0:T(8,128)(2,1)S(1)} collective-permute-done((bf16[256,512]{1,0:T(8,128)(2,1)S(1)}, bf16[256,512]{1,0:T(8,128)(2,1)S(1)}, u32[]{:S(2)}, u32[]{:S(2)}) %collective-permute-start.1) | collective-permute-done | bytes 262176 | tf_op jit(solution)/shard_map/ppermute | solution.py:287
  27.1 4.7 %collective-permute-start.3 = (bf16[128,512]{1,0:T(8,128)(2,1)S(1)}, bf16[128,512]{1,0:T(8,128)(2,1)S(1)}, u32[]{:S(2)}, u32[]{:S(2)}) collective-permute-start(bf16[128,512]{1,0:T(8,128)(2,1)S(1)} %slice.13), channel_id=1, source_target_pairs={{0,96},{16,112},{32,0},{48,16},{64,32},{80,48},{96,64},{112,80},{1... | collective-permute-start | bytes 393224 | tf_op jit(solution)/shard_map/ppermute | solution.py:287
  31.7 0.0 collective-permute-done.refs_1_
  31.8 0.1 collective-permute-start.2
  31.8 0.1 collective-permute-start.4
  32.0 0.0 copy-start.1
  32.0 0.0 copy-start.3
  32.0 0.5 collective-permute-start.6
  32.5 0.1 collective-permute-start.5
  32.6 3.5 %collective-permute-done.3.refs_4_ = bf16[128,512]{1,0:T(8,128)(2,1)S(1)} collective-permute-done((bf16[128,512]{1,0:T(8,128)(2,1)S(1)}, bf16[128,512]{1,0:T(8,128)(2,1)S(1)}, u32[]{:S(2)}, u32[]{:S(2)}) %collective-permute-start.3) | collective-permute-done | bytes 131104 | tf_op jit(solution)/shard_map/ppermute | solution.py:287
  36.1 0.0 collective-permute-start.8
  36.1 4.1 %collective-permute-done.2.refs_3_ = bf16[128,512]{1,0:T(8,128)(2,1)S(1)} collective-permute-done((bf16[128,512]{1,0:T(8,128)(2,1)S(1)}, bf16[128,512]{1,0:T(8,128)(2,1)S(1)}, u32[]{:S(2)}, u32[]{:S(2)}) %collective-permute-start.2) | collective-permute-done | bytes 131104 | tf_op jit(solution)/shard_map/ppermute | solution.py:287
  40.2 0.0 collective-permute-start.7
  40.2 0.0 all-to-all-done.signal_ref
  40.2 5.3 %convolve.1 = (f32[16,16,512]{2,1,0:T(8,128)}, f32[2,512,256]{2,1,0:T(8,128)}) custom-call(f32[16,16,512]{2,1,0:T(8,128)} %all-to-all-done.signal_ref, f32[16,8192]{1,0:T(8,128)} %filt_ref.1, bf16[128,192]{1,0:T(8,128)(2,1)} %constant.28.clone.natural_ref, bf16[128,192]{1,0:T(8,128)(2,1)} %constant.23.clone.analyse_ref, ...), custom_call_target="tpu_custom_call" | custom-call | flops 4000000000 | bytes 3000000 | tf_op jit(solution)/shard_map/convolve/pallas_call | solution.py:248
  45.5 0.0 collective-permute-done.4.refs_5_
  45.5 0.0 collective-permute-done.8.refs_9_
  45.5 0.0 collective-permute-done.6.refs_7_
  45.5 0.0 collective-permute-done.7.refs_8_
  45.6 0.0 collective-permute-done.5.refs_6_
  45.6 0.0 copy-done.1
  45.6 0.0 copy-done.3
  45.6 1.7 %shard_map.147 = (f32[16,16,1024]{2,1,0:T(8,128)S(1)}, f32[256,512]{1,0:T(8,128)S(1)}) custom-call(s32[1]{0:T(128)} %bitcast.place_ref, f32[16,16,512]{2,1,0:T(8,128)} %get-tuple-element.11.conv_ref, bf16[256,512]{1,0:T(8,128)(2,1)S(1)} %bitcast.15, bf16[256,2048]{1,0:T(8,128)(2,1)S(1)} %copy-done.3, bf16[256,512]{1,0:T(8,128)(2,1)S(1)} %bitcast.20, ...), custom_call_target="tpu_custom_call" | custom-call | flops 600000000 | bytes 5000000 | tf_op jit(solution)/shard_map/pallas_call | solution.py:330
  47.3 0.0 copy-start.4
  47.3 23.5 %all_to_all.20.both_ref.signal_ref = f32[16,16,1024]{2,1,0:T(8,128)S(1)} all-to-all(f32[16,16,1024]{2,1,0:T(8,128)S(1)} %get-tuple-element.13), channel_id=1, replica_groups=mesh['dp'=2,'chan'=8,'seq'=16] {'seq'}, dimensions={0} | all-to-all | bytes 2097152 | tf_op jit(solution)/shard_map/all_to_all | solution.py:305
  70.8 0.9 shard_map.148
  71.7 0.0 copy-done.4
  71.7 0.0 copy-done
  71.8 19.8 %all_to_all.21.refs_0_ = bf16[32,8,2048]{2,1,0:T(8,128)(2,1)S(1)} all-to-all(bf16[32,8,2048]{2,1,0:T(8,128)(2,1)S(1)} %bitcast.14), channel_id=1, replica_groups=mesh['dp'=2,'chan'=8,'seq'=16] {'dp','seq'}, dimensions={0} | all-to-all | bytes 2097152 | tf_op jit(solution)/shard_map/all_to_all | solution.py:305
  91.5 0.2 total.1.mine_ref
  91.7 1.5 %collective-permute-start.9 = (bf16[16,1024]{1,0:T(8,128)(2,1)S(1)}, bf16[16,1024]{1,0:T(8,128)(2,1)S(1)}, u32[]{:S(2)}, u32[]{:S(2)}) collective-permute-start(bf16[16,1024]{1,0:T(8,128)(2,1)S(1)} %total.1.mine_ref), channel_id=1, source_target_pairs={{0,128},{128,0},{1,129},{129,1},{2,130},{130,2},{3,131},{131,3},{4... | collective-permute-start | bytes 98312 | tf_op jit(solution)/shard_map/ppermute | solution.py:356
  93.1 5.5 %correlate.1.back_ref = bf16[16,48,1024]{2,1,0:T(8,128)(2,1)} custom-call(f32[16,16,1024]{2,1,0:T(8,128)} %copy-done, f32[2,512,256]{2,1,0:T(8,128)} %get-tuple-element.14.spec_ref, bf16[128,192]{1,0:T(8,128)(2,1)} %constant.23.clone.analyse_ref, bf16[64,384]{1,0:T(8,128)(2,1)} %constant.24.clone.restore_ref, f32[2,64,128]{2,1,0:T(8,128)} %constant.25.clone.twist_ref, ...), custom_call_target="tpu_custom_call" | custom-call | flops 4000000000 | bytes 3000000 | tf_op jit(solution)/shard_map/correlate/pallas_call | solution.py:262
  98.6 0.0 collective-permute-done.9.other_ref
  98.6 1.2 last.1
  99.8 0.0 slice-start
  99.8 0.0 copy-start.5
  99.9 5.4 %all-to-all-start.3 = ((bf16[16,48,1024]{2,1,0:T(8,128)(2,1)}), bf16[16,48,1024]{2,1,0:T(8,128)(2,1)S(1)}, u32[]{:S(2)}, u32[]{:S(2)}) async-start(bf16[16,48,1024]{2,1,0:T(8,128)(2,1)} %last.1), calls=%async_computation.3 | async-start | bytes 3145728 | tf_op jit(solution)/shard_map/all_to_all | solution.py:305
  105.3 0.0 copy-start.7
  105.3 0.8 fusion
  106.1 20.0 %all-to-all-done.3.all_ref = bf16[16,48,1024]{2,1,0:T(8,128)(2,1)S(1)} async-done(((bf16[16,48,1024]{2,1,0:T(8,128)(2,1)}), bf16[16,48,1024]{2,1,0:T(8,128)(2,1)S(1)}, u32[]{:S(2)}, u32[]{:S(2)}) %all-to-all-start.3) | async-done | bytes 1572896 | tf_op jit(solution)/shard_map/all_to_all | solution.py:305
  126.1 0.0 copy-done.6
  126.1 1.7 %shard_map.149 = (bf16[256,512]{1,0:T(8,128)(2,1)}, bf16[256,512]{1,0:T(8,128)(2,1)}, f32[256,2048]{1,0:T(8,128)}) custom-call(s32[1]{0:T(128)} %bitcast.7.dp_ref, bf16[16,48,1024]{2,1,0:T(8,128)(2,1)S(1)} %all-to-all-done.3.all_ref, bf16[256,512]{1,0:T(8,128)(2,1)S(1)} %bitcast.23, bf16[256,512]{1,0:T(8,128)(2,1)S(1)} %bitcast.25), custom_call_target="tpu_custom_call" | custom-call | flops 600000000 | bytes 5000000 | tf_op jit(solution)/shard_map/pallas_call | solution.py:370
  (7 shorter events, 0.0 us)
Async XLA Ops:
  0.6 9.4 %copy-start.2 = (bf16[1,256,512]{2,1,0:T(8,128)(2,1)S(1)}, bf16[1,256,512]{2,1,0:T(8,128)(2,1)}, u32[]{:S(2)}) copy-start(bf16[1,256,512]{2,1,0:T(8,128)(2,1)} %param.15) | copy-start | bytes 786436
  2.6 37.6 %all-to-all-start = ((f32[16,16,512]{2,1,0:T(8,128)}), f32[16,16,512]{2,1,0:T(8,128)}, u32[]{:S(2)}, u32[]{:S(2)}) async-start(f32[16,16,512]{2,1,0:T(8,128)} %mix.1), calls=%async_computation | async-start | bytes 1048576 | tf_op jit(solution)/shard_map/all_to_all | solution.py:305
  10.0 17.0 %collective-permute-start.1 = (bf16[256,512]{1,0:T(8,128)(2,1)S(1)}, bf16[256,512]{1,0:T(8,128)(2,1)S(1)}, u32[]{:S(2)}, u32[]{:S(2)}) collective-permute-start(bf16[256,512]{1,0:T(8,128)(2,1)S(1)} %bitcast.17), channel_id=1, source_target_pairs={{0,96},{16,112},{32,0},{48,16},{64,32},{80,48},{96,64},{112,80},{1... | collective-permute-start | bytes 786440 | tf_op jit(solution)/shard_map/ppermute | solution.py:287
  16.4 15.3 %collective-permute-start = (bf16[256,512]{1,0:T(8,128)(2,1)S(1)}, bf16[256,512]{1,0:T(8,128)(2,1)S(1)}, u32[]{:S(2)}, u32[]{:S(2)}) collective-permute-start(bf16[256,512]{1,0:T(8,128)(2,1)S(1)} %bitcast.18), channel_id=1, source_target_pairs={{0,32},{16,48},{32,64},{48,80},{64,96},{80,112},{96,0},{112,16},{1... | collective-permute-start | bytes 786440 | tf_op jit(solution)/shard_map/ppermute | solution.py:287
  27.1 9.0 %collective-permute-start.3 = (bf16[128,512]{1,0:T(8,128)(2,1)S(1)}, bf16[128,512]{1,0:T(8,128)(2,1)S(1)}, u32[]{:S(2)}, u32[]{:S(2)}) collective-permute-start(bf16[128,512]{1,0:T(8,128)(2,1)S(1)} %slice.13), channel_id=1, source_target_pairs={{0,96},{16,112},{32,0},{48,16},{64,32},{80,48},{96,64},{112,80},{1... | collective-permute-start | bytes 393224 | tf_op jit(solution)/shard_map/ppermute | solution.py:287
  31.8 8.4 %collective-permute-start.2 = (bf16[128,512]{1,0:T(8,128)(2,1)S(1)}, bf16[128,512]{1,0:T(8,128)(2,1)S(1)}, u32[]{:S(2)}, u32[]{:S(2)}) collective-permute-start(bf16[128,512]{1,0:T(8,128)(2,1)S(1)} %slice.12), channel_id=1, source_target_pairs={{0,32},{16,48},{32,64},{48,80},{64,96},{80,112},{96,0},{112,16},{1... | collective-permute-start | bytes 393224 | tf_op jit(solution)/shard_map/ppermute | solution.py:287
  31.8 13.7 %collective-permute-start.4 = (bf16[256,512]{1,0:T(8,128)(2,1)S(1)}, bf16[256,512]{1,0:T(8,128)(2,1)S(1)}, u32[]{:S(2)}, u32[]{:S(2)}) collective-permute-start(bf16[256,512]{1,0:T(8,128)(2,1)S(1)} %bitcast.19), channel_id=1, source_target_pairs={{0,16},{16,0},{32,48},{48,32},{64,80},{80,64},{96,112},{112,96},{1... | collective-permute-start | bytes 786440 | tf_op jit(solution)/shard_map/ppermute | solution.py:287
  32.0 13.6 %copy-start.1 = (bf16[1,256,512]{2,1,0:T(8,128)(2,1)S(1)}, bf16[1,256,512]{2,1,0:T(8,128)(2,1)}, u32[]{:S(2)}) copy-start(bf16[1,256,512]{2,1,0:T(8,128)(2,1)} %param.12) | copy-start | bytes 786436
  32.0 13.6 %copy-start.3 = (bf16[256,2048]{1,0:T(8,128)(2,1)S(1)}, bf16[256,2048]{1,0:T(8,128)(2,1)}, u32[]{:S(2)}) copy-start(bf16[256,2048]{1,0:T(8,128)(2,1)} %weight_ref.1) | copy-start | bytes 3145732
  32.0 13.6 %collective-permute-start.6 = (bf16[256,512]{1,0:T(8,128)(2,1)S(1)}, bf16[256,512]{1,0:T(8,128)(2,1)S(1)}, u32[]{:S(2)}, u32[]{:S(2)}) collective-permute-start(bf16[256,512]{1,0:T(8,128)(2,1)S(1)} %collective-permute-done.1.refs_2_), channel_id=1, source_target_pairs={{0,16},{16,0},{32,48},{48,32},{64,80},{80,64},{96,112},{112,96},{1... | collective-permute-start | bytes 786440 | tf_op jit(solution)/shard_map/ppermute | solution.py:287
  32.5 13.1 %collective-permute-start.5 = (bf16[256,512]{1,0:T(8,128)(2,1)S(1)}, bf16[256,512]{1,0:T(8,128)(2,1)S(1)}, u32[]{:S(2)}, u32[]{:S(2)}) collective-permute-start(bf16[256,512]{1,0:T(8,128)(2,1)S(1)} %collective-permute-done.refs_1_), channel_id=1, source_target_pairs={{0,16},{16,0},{32,48},{48,32},{64,80},{80,64},{96,112},{112,96},{1... | collective-permute-start | bytes 786440 | tf_op jit(solution)/shard_map/ppermute | solution.py:287
  36.1 9.4 %collective-permute-start.8 = (bf16[128,512]{1,0:T(8,128)(2,1)S(1)}, bf16[128,512]{1,0:T(8,128)(2,1)S(1)}, u32[]{:S(2)}, u32[]{:S(2)}) collective-permute-start(bf16[128,512]{1,0:T(8,128)(2,1)S(1)} %collective-permute-done.3.refs_4_), channel_id=1, source_target_pairs={{0,16},{16,0},{32,48},{48,32},{64,80},{80,64},{96,112},{112,96},{1... | collective-permute-start | bytes 393224 | tf_op jit(solution)/shard_map/ppermute | solution.py:287
  40.2 5.4 %collective-permute-start.7 = (bf16[128,512]{1,0:T(8,128)(2,1)S(1)}, bf16[128,512]{1,0:T(8,128)(2,1)S(1)}, u32[]{:S(2)}, u32[]{:S(2)}) collective-permute-start(bf16[128,512]{1,0:T(8,128)(2,1)S(1)} %collective-permute-done.2.refs_3_), channel_id=1, source_target_pairs={{0,16},{16,0},{32,48},{48,32},{64,80},{80,64},{96,112},{112,96},{1... | collective-permute-start | bytes 393224 | tf_op jit(solution)/shard_map/ppermute | solution.py:287
  47.3 24.5 %copy-start.4 = (f32[256,512]{1,0:T(8,128)}, f32[256,512]{1,0:T(8,128)S(1)}, u32[]{:S(2)}) copy-start(f32[256,512]{1,0:T(8,128)S(1)} %get-tuple-element.12) | copy-start | bytes 1572868
  70.8 1.0 copy-start
  91.7 6.9 %collective-permute-start.9 = (bf16[16,1024]{1,0:T(8,128)(2,1)S(1)}, bf16[16,1024]{1,0:T(8,128)(2,1)S(1)}, u32[]{:S(2)}, u32[]{:S(2)}) collective-permute-start(bf16[16,1024]{1,0:T(8,128)(2,1)S(1)} %total.1.mine_ref), channel_id=1, source_target_pairs={{0,128},{128,0},{1,129},{129,1},{2,130},{130,2},{3,131},{131,3},{4... | collective-permute-start | bytes 98312 | tf_op jit(solution)/shard_map/ppermute | solution.py:356
  99.8 5.5 %slice-start = ((f32[16,16,1024]{2,1,0:T(8,128)}), f32[16,16,512]{2,1,0:T(8,128)S(1)}, s32[]{:S(2)}) async-start(f32[16,16,1024]{2,1,0:T(8,128)} %copy-done), calls=%async_computation.4 | async-start | bytes 1048576 | tf_op jit(solution)/shard_map/slice | solution.py:343
  99.8 5.5 %copy-start.5 = (f32[256,512]{1,0:T(8,128)S(1)}, f32[256,512]{1,0:T(8,128)}, u32[]{:S(2)}) copy-start(f32[256,512]{1,0:T(8,128)} %copy-done.4) | copy-start | bytes 1572868
  99.9 26.3 %all-to-all-start.3 = ((bf16[16,48,1024]{2,1,0:T(8,128)(2,1)}), bf16[16,48,1024]{2,1,0:T(8,128)(2,1)S(1)}, u32[]{:S(2)}, u32[]{:S(2)}) async-start(bf16[16,48,1024]{2,1,0:T(8,128)(2,1)} %last.1), calls=%async_computation.3 | async-start | bytes 3145728 | tf_op jit(solution)/shard_map/all_to_all | solution.py:305
  105.3 20.9 %copy-start.6 = (bf16[1,256,512]{2,1,0:T(8,128)(2,1)S(1)}, bf16[1,256,512]{2,1,0:T(8,128)(2,1)}, u32[]{:S(2)}) copy-start(bf16[1,256,512]{2,1,0:T(8,128)(2,1)} %param.13) | copy-start | bytes 786436
  105.3 20.9 %copy-start.7 = (bf16[1,256,512]{2,1,0:T(8,128)(2,1)S(1)}, bf16[1,256,512]{2,1,0:T(8,128)(2,1)}, u32[]{:S(2)}) copy-start(bf16[1,256,512]{2,1,0:T(8,128)(2,1)} %param.14) | copy-start | bytes 786436

commit v2 on v1

--- a/solution.py
+++ b/solution.py
@@ -13,7 +13,7 @@
 WIDE = 128
 TALL = 64
 LIMIT = 20
-BATCH = 8
+BATCH = 16
 
 
 def split_table(values):
@@ -115,29 +115,33 @@
     )
 
 
-def convolve_kernel(signal_ref, filt_ref, natural_ref, analyse_ref, restore_ref, twist_ref, there_ref, back_ref, out_ref, spec_ref, rows_ref):
+def convolve_kernel(signal_ref, filt_ref, natural_ref, analyse_ref, restore_ref, twist_ref, there_ref, back_ref, out_ref, spec_ref, taps_ref, rows_ref):
     twist = twist_ref[...]
-    blocks, channels, width = out_ref.shape
+    blocks, channels, width = signal_ref.shape
     for place in range(TALL):
-        rows_ref[place] = filt_ref[:, place * WIDE : (place + 1) * WIDE]
+        taps_ref[place] = filt_ref[:, place * WIDE : (place + 1) * WIDE]
     for group in range(channels // BATCH):
         members = range(group * BATCH, (group + 1) * BATCH)
-        filt = forward_group([rows_ref[:, m, :] for m in members], natural_ref[...], twist, there_ref[...])
+        filt = forward_group([taps_ref[:, m, :] for m in members], natural_ref[...], twist, there_ref[...])
         spec_ref[group] = filt
         inputs = [arrived_rows(signal_ref, m, 0, width) for m in members]
         spec = forward_group(inputs, analyse_ref[...], twist, there_ref[...])
         result = inverse_group(product(spec, filt, False), restore_ref[...], twist, back_ref[...])
         for which, m in enumerate(members):
-            out_ref[:, m, :] = sent_rows(result, which, blocks)
-
-
-def correlate_kernel(signal_ref, spec_ref, analyse_ref, restore_ref, twist_ref, there_ref, back_ref, out_ref, rows_ref):
+            rows_ref[:, m, :] = sent_rows(result, which, blocks)
+    high, low = halves(rows_ref[...])
+    out_ref[:, :, :width] = high
+    out_ref[:, :, width:] = low
+
+
+def correlate_kernel(both_ref, spec_ref, analyse_ref, restore_ref, twist_ref, there_ref, back_ref, out_ref, signal_ref, rows_ref):
     twist = twist_ref[...]
     blocks, channels, width = rows_ref.shape
     below = out_ref.shape[1] - channels
+    signal_ref[...] = both_ref[:, :, 2 * width :].astype(jnp.float32)
     for group in range(channels // BATCH):
         members = range(group * BATCH, (group + 1) * BATCH)
-        inputs = [arrived_rows(signal_ref, m, width, width) for m in members]
+        inputs = [arrived_rows(signal_ref, m, 0, width) for m in members]
         spec = forward_group(inputs, analyse_ref[...], twist, there_ref[...])
         result = inverse_group(product(spec, spec_ref[group], True), restore_ref[...], twist, back_ref[...])
         for which, m in enumerate(members):
@@ -179,7 +183,7 @@
         total = term if total is None else total + term
     mid_ref[...] = total
     gate = query_ref[...].astype(jnp.float32) * total
-    both_ref[:, :, width:] = gate.reshape(seqs, rows, width)
+    both_ref[:, :, width:] = gate.astype(jnp.bfloat16).reshape(seqs, rows, width // 2)
     copy.wait()
 
 
@@ -187,7 +191,8 @@
     blocks, (part_ref,) = refs[:10], refs[10:]
     step = blocks[0].shape[0]
     channels, width = query_ref.shape
-    conv_out = both_ref[:, :, :width].reshape(channels, width)
+    both = both_ref[:, :, : 2 * width].astype(jnp.float32)
+    conv_out = (both[:, :, :width] + both[:, :, width:]).reshape(channels, width)
     gated = (query_ref[...].astype(jnp.float32) * conv_out).astype(jnp.bfloat16)
     for (start, size), block in zip(places(place_ref, step), blocks):
         term = lax.dot_general(
@@ -239,30 +244,39 @@
         grad_value_ref[place, :] = (mixed * key_ref[place, :].astype(jnp.float32)).astype(jnp.bfloat16)
 
 
+def fixed(values):
+    return pltpu.with_memory_space_constraint(values, pltpu.HBM)
+
+
 def limited(mebibytes):
     return pltpu.CompilerParams(vmem_limit_bytes=mebibytes * 1024 * 1024)
 
 
 def convolve(signal, filt, natural, tables):
-    _, channels, _ = signal.shape
+    blocks, channels, width = signal.shape
     return pl.pallas_call(
         convolve_kernel,
         out_shape=(
-            jax.ShapeDtypeStruct(signal.shape, jnp.float32),
+            jax.ShapeDtypeStruct((blocks, channels, 2 * width), jnp.bfloat16),
             jax.ShapeDtypeStruct((channels // BATCH, BATCH * TALL, 2 * WIDE), jnp.float32),
         ),
-        scratch_shapes=[pltpu.VMEM((TALL, channels, WIDE), jnp.float32)],
+        scratch_shapes=[
+            pltpu.VMEM((TALL, channels, WIDE), jnp.float32),
+            pltpu.VMEM(signal.shape, jnp.float32),
+        ],
         name="convolve",
+        compiler_params=limited(40),
         cost_estimate=pl.CostEstimate(flops=4_000_000_000, bytes_accessed=3_000_000, transcendentals=0),
     )(signal, filt, natural, *tables)
 
 
 def correlate(both, spec, tables, above):
-    blocks, channels, double = both.shape
+    blocks, channels, triple = both.shape
+    width = triple // 3
     return pl.pallas_call(
         correlate_kernel,
-        out_shape=jax.ShapeDtypeStruct((blocks, above + channels, double), jnp.bfloat16),
-        scratch_shapes=[pltpu.VMEM((blocks, channels, double // 2), jnp.float32)],
+        out_shape=jax.ShapeDtypeStruct((blocks, above + channels, 2 * width), jnp.bfloat16),
+        scratch_shapes=[pltpu.VMEM((blocks, channels, width), jnp.float32)] * 2,
         name="correlate",
         cost_estimate=pl.CostEstimate(flops=4_000_000_000, bytes_accessed=3_000_000, transcendentals=0),
     )(both, spec, *tables)
@@ -315,7 +329,7 @@
     twist, there, back = make_shared()
     analyse_natural, _ = make_tables(np.arange(TALL))
     analyse, restore = make_tables(arrived)
-    tables = tuple(jnp.asarray(t) for t in (analyse, restore, twist, there, back))
+    tables = tuple(fixed(jnp.asarray(t)) for t in (analyse, restore, twist, there, back))
     place = lax.axis_index("chan").astype(jnp.int32).reshape(1)
 
     blocks = gather_features(grad_out[0], chans)
@@ -325,22 +339,23 @@
         name="mix",
     )(key_proj[0], value_proj[0])
     mixed_full = swap(mixed_in)
-    conv_full, spec = convolve(mixed_full, long_filter, jnp.asarray(analyse_natural), tables)
+    conv_full, spec = convolve(mixed_full, fixed(long_filter), fixed(jnp.asarray(analyse_natural)), tables)
 
     both, grad_mid = placed_call(
         gate_kernel,
         13,
         (
-            jax.ShapeDtypeStruct((seqs, rows, 2 * span), jnp.float32),
+            jax.ShapeDtypeStruct((seqs, rows, 3 * span), jnp.bfloat16),
             jax.ShapeDtypeStruct((channels, span), jnp.float32),
         ),
         left=(0,),
-    )(place, pltpu.with_memory_space_constraint(conv_full, pltpu.HBM), query_proj[0], out_weight, *blocks)
+    )(place, fixed(conv_full), query_proj[0], out_weight, *blocks)
     both = swap(both)
     weight_part = placed_call(
         part_kernel, 12, jax.ShapeDtypeStruct((channels, features), jnp.bfloat16)
     )(place, both, query_proj[0], *blocks)
-    grad_query = (grad_mid * both[:, :, :span].reshape(channels, span)).astype(jnp.bfloat16)
+    conv_out = both[:, :, :span].astype(jnp.float32) + both[:, :, span : 2 * span].astype(jnp.float32)
+    grad_query = (grad_mid * conv_out.reshape(channels, span)).astype(jnp.bfloat16)
 
     group = dps * seqs
     weight_part = swap(weight_part.reshape(group, channels // group, features), ("dp", "seq"))
@@ -365,7 +380,7 @@
         scratch_shapes=[pltpu.SemaphoreType.DMA((seqs, 2))],
         name="last",
         compiler_params=limited(LIMIT),
-    )(mine, other, pltpu.with_memory_space_constraint(back_full, pltpu.HBM))
+    )(mine, other, fixed(back_full))
     last = swap(last)
     grad_key, grad_value, grad_weight = placed_call(
         final_kernel,

time: 129 us -> 127 us (0.984)
  the two profiles are of different devices: /device:TPU:2 before, /device:TPU:64 now
where the time goes in v2:
time: 127 us; the launch traced here: 126 us
  blocking collectives  41.4 us (33%)
  waiting for transfers between devices  40.8 us (32%)
  starting transfers between devices  22.9 us (18%)
  Pallas kernels  17 us (13%)
  local copies, waits for them, and re-layouts  2.41 us (2%)
    all_to_all x2, blocking collectives, swap(): return lax.all_to_all(blocks, axes, split_axis=0, concat_axis=0, tiled=True)  41.4 us
    all_to_all x2, waiting for transfers between devices, swap(): return lax.all_to_all(blocks, axes, split_axis=0, concat_axis=0, tiled=True)  22.5 us
    ppermute x9, waiting for transfers between devices, send(): return lax.ppermute(values, 'chan', [(k, hop(k)) for k in range(chans)])  18.3 us
    all_to_all x2, starting transfers between devices, swap(): return lax.all_to_all(blocks, axes, split_axis=0, concat_axis=0, tiled=True)  11.2 us
    ppermute x9, starting transfers between devices, send(): return lax.ppermute(values, 'chan', [(k, hop(k)) for k in range(chans)])  10 us
    pallas_call x1, Pallas kernels, correlate(): pl.pallas_call(correlate_kernel, out_shape=jax.ShapeDtypeStruct((blocks,...  5.03 us
    pallas_call x1, Pallas kernels, convolve(): pl.pallas_call(convolve_kernel, out_shape=(jax.ShapeDtypeStruct((blocks,...  4.36 us
  transfers between devices with their start and end apart: 12, of which 4 were waited for; matrix products, arithmetic and copies ran while one was open for 1% of the time, Pallas kernels for 7%

profile of v2, /device:TPU:64, one launch (start us, length us, event | category | flops | bytes accessed | tf_op | source)
XLA Modules:
  0.0 126.2 jit_solution(6911365093746024243)
XLA Ops:
  0.6 0.0 copy-start.3
  0.6 1.9 %mix.1 = f32[16,16,512]{2,1,0:T(8,128)} custom-call(bf16[256,512]{1,0:T(8,128)(2,1)} %bitcast.22, bf16[256,512]{1,0:T(8,128)(2,1)} %bitcast.24), custom_call_target="tpu_custom_call" | custom-call | tf_op jit(solution)/shard_map/mix/pallas_call | solution.py:336
  2.6 7.0 %all-to-all-start = ((f32[16,16,512]{2,1,0:T(8,128)}), f32[16,16,512]{2,1,0:T(8,128)S(1)}, u32[]{:S(2)}, u32[]{:S(2)}) async-start(f32[16,16,512]{2,1,0:T(8,128)} %mix.1), calls=%async_computation | async-start | bytes 1048576 | tf_op jit(solution)/shard_map/all_to_all | solution.py:319
  9.6 0.0 copy-done.3
  9.6 4.6 %collective-permute-start = (bf16[256,512]{1,0:T(8,128)(2,1)S(1)}, bf16[256,512]{1,0:T(8,128)(2,1)S(1)}, u32[]{:S(2)}, u32[]{:S(2)}) collective-permute-start(bf16[256,512]{1,0:T(8,128)(2,1)S(1)} %bitcast.17), channel_id=1, source_target_pairs={{0,32},{16,48},{32,64},{48,80},{64,96},{80,112},{96,0},{112,16},{1... | collective-permute-start | bytes 786440 | tf_op jit(solution)/shard_map/ppermute | solution.py:301
  14.2 0.0 collective-permute-start.1
  14.2 10.8 %collective-permute-done.refs_1_ = bf16[256,512]{1,0:T(8,128)(2,1)S(1)} collective-permute-done((bf16[256,512]{1,0:T(8,128)(2,1)S(1)}, bf16[256,512]{1,0:T(8,128)(2,1)S(1)}, u32[]{:S(2)}, u32[]{:S(2)}) %collective-permute-start) | collective-permute-done | bytes 262176 | tf_op jit(solution)/shard_map/ppermute | solution.py:301
  25.0 4.7 %collective-permute-start.2 = (bf16[128,512]{1,0:T(8,128)(2,1)S(1)}, bf16[128,512]{1,0:T(8,128)(2,1)S(1)}, u32[]{:S(2)}, u32[]{:S(2)}) collective-permute-start(bf16[128,512]{1,0:T(8,128)(2,1)S(1)} %slice.16), channel_id=1, source_target_pairs={{0,32},{16,48},{32,64},{48,80},{64,96},{80,112},{96,0},{112,16},{1... | collective-permute-start | bytes 393224 | tf_op jit(solution)/shard_map/ppermute | solution.py:301
  29.7 0.0 collective-permute-done.1.refs_2_
  29.7 0.1 collective-permute-start.3
  29.8 0.1 collective-permute-start.4
  29.9 0.0 copy-start.2
  29.9 0.5 collective-permute-start.5
  30.4 0.1 collective-permute-start.6
  30.5 3.6 %collective-permute-done.2.refs_3_ = bf16[128,512]{1,0:T(8,128)(2,1)S(1)} collective-permute-done((bf16[128,512]{1,0:T(8,128)(2,1)S(1)}, bf16[128,512]{1,0:T(8,128)(2,1)S(1)}, u32[]{:S(2)}, u32[]{:S(2)}) %collective-permute-start.2) | collective-permute-done | bytes 131104 | tf_op jit(solution)/shard_map/ppermute | solution.py:301
  34.1 0.0 collective-permute-start.7
  34.1 3.9 %collective-permute-done.3.refs_4_ = bf16[128,512]{1,0:T(8,128)(2,1)S(1)} collective-permute-done((bf16[128,512]{1,0:T(8,128)(2,1)S(1)}, bf16[128,512]{1,0:T(8,128)(2,1)S(1)}, u32[]{:S(2)}, u32[]{:S(2)}) %collective-permute-start.3) | collective-permute-done | bytes 131104 | tf_op jit(solution)/shard_map/ppermute | solution.py:301
  38.0 0.0 collective-permute-start.8
  38.0 0.0 all-to-all-done.signal_ref
  38.0 4.4 %convolve.1 = (bf16[16,16,1024]{2,1,0:T(8,128)(2,1)S(1)}, f32[1,1024,256]{2,1,0:T(8,128)S(1)}) custom-call(f32[16,16,512]{2,1,0:T(8,128)S(1)} %all-to-all-done.signal_ref, f32[16,8192]{1,0:T(8,128)} %filt_ref.1, bf16[128,192]{1,0:T(8,128)(2,1)} %constant.28.clone.natural_ref, bf16[128,192]{1,0:T(8,128)(2,1)} %constant.23.clone.analyse_ref, ...), custom_call_target="tpu_custom_call" | custom-call | flops 4000000000 | bytes 3000000 | tf_op jit(solution)/shard_map/convolve/pallas_call | solution.py:257
  42.4 0.0 copy-start.5
  42.4 0.8 copy-done.5
  43.2 0.0 collective-permute-done.4.refs_5_
  43.2 0.0 collective-permute-done.5.refs_6_
  43.2 0.0 collective-permute-done.6.refs_7_
  43.2 0.0 collective-permute-done.7.refs_8_
  43.2 0.0 collective-permute-done.8.refs_9_
  43.2 0.0 copy-done.2
  43.2 0.0 copy-start.4
  43.2 1.6 %copy-done.4 = bf16[256,2048]{1,0:T(8,128)(2,1)S(1)} copy-done((bf16[256,2048]{1,0:T(8,128)(2,1)S(1)}, bf16[256,2048]{1,0:T(8,128)(2,1)}, u32[]{:S(2)}) %copy-start.4) | copy-done | bytes 1048600
  44.8 1.7 %shard_map.147 = (bf16[16,16,1536]{2,1,0:T(8,128)(2,1)S(1)}, f32[256,512]{1,0:T(8,128)S(1)}) custom-call(s32[1]{0:T(128)} %bitcast.place_ref, bf16[16,16,1024]{2,1,0:T(8,128)(2,1)} %copy-done.5, bf16[256,512]{1,0:T(8,128)(2,1)S(1)} %bitcast.15, bf16[256,2048]{1,0:T(8,128)(2,1)S(1)} %copy-done.4, bf16[256,512]{1,0:T(8,128)(2,1)S(1)} %bitcast.20, ...), custom_call_target="tpu_custom_call" | custom-call | flops 600000000 | bytes 5000000 | tf_op jit(solution)/shard_map/pallas_call | solution.py:344
  46.4 0.0 copy-done.10
  46.5 21.8 %all_to_all.20.both_ref = bf16[16,16,1536]{2,1,0:T(8,128)(2,1)S(1)} all-to-all(bf16[16,16,1536]{2,1,0:T(8,128)(2,1)S(1)} %get-tuple-element.13), channel_id=1, replica_groups=mesh['dp'=2,'chan'=8,'seq'=16] {'seq'}, dimensions={0} | all-to-all | bytes 1572864 | tf_op jit(solution)/shard_map/all_to_all | solution.py:319
  68.3 0.9 shard_map.148
  69.3 19.5 %all_to_all.21.refs_0_ = bf16[32,8,2048]{2,1,0:T(8,128)(2,1)S(1)} all-to-all(bf16[32,8,2048]{2,1,0:T(8,128)(2,1)S(1)} %bitcast.14), channel_id=1, replica_groups=mesh['dp'=2,'chan'=8,'seq'=16] {'dp','seq'}, dimensions={0} | all-to-all | bytes 2097152 | tf_op jit(solution)/shard_map/all_to_all | solution.py:319
  88.8 0.2 total.1.mine_ref
  89.0 1.7 %collective-permute-start.9 = (bf16[16,1024]{1,0:T(8,128)(2,1)S(1)}, bf16[16,1024]{1,0:T(8,128)(2,1)S(1)}, u32[]{:S(2)}, u32[]{:S(2)}) collective-permute-start(bf16[16,1024]{1,0:T(8,128)(2,1)S(1)} %total.1.mine_ref), channel_id=1, source_target_pairs={{0,128},{128,0},{1,129},{129,1},{2,130},{130,2},{3,131},{131,3},{4... | collective-permute-start | bytes 98312 | tf_op jit(solution)/shard_map/ppermute | solution.py:371
  90.7 5.0 %correlate.1.back_ref = bf16[16,48,1024]{2,1,0:T(8,128)(2,1)} custom-call(bf16[16,16,1536]{2,1,0:T(8,128)(2,1)} %copy-done, f32[1,1024,256]{2,1,0:T(8,128)} %copy-done.10, bf16[128,192]{1,0:T(8,128)(2,1)} %constant.23.clone.analyse_ref, bf16[64,384]{1,0:T(8,128)(2,1)} %constant.24.clone.restore_ref, f32[2,64,128]{2,1,0:T(8,128)} %constant.25.clone.twist_ref, ...), custom_call_target="tpu_custom_call" | custom-call | flops 4000000000 | bytes 3000000 | tf_op jit(solution)/shard_map/correlate/pallas_call | solution.py:276
  95.7 0.0 collective-permute-done.9.other_ref
  95.7 1.2 last.1
  96.9 4.1 %all-to-all-start.3 = ((bf16[16,48,1024]{2,1,0:T(8,128)(2,1)}), bf16[16,48,1024]{2,1,0:T(8,128)(2,1)S(1)}, u32[]{:S(2)}, u32[]{:S(2)}) async-start(bf16[16,48,1024]{2,1,0:T(8,128)(2,1)} %last.1), calls=%async_computation.3 | async-start | bytes 3145728 | tf_op jit(solution)/shard_map/all_to_all | solution.py:319
  101.1 0.0 copy-start.8
  101.1 0.0 copy-start.9
  101.1 0.0 copy-done.1
  101.1 0.1 convert_add_fusion
  101.2 0.8 fusion
  102.0 22.5 %all-to-all-done.3.all_ref = bf16[16,48,1024]{2,1,0:T(8,128)(2,1)S(1)} async-done(((bf16[16,48,1024]{2,1,0:T(8,128)(2,1)}), bf16[16,48,1024]{2,1,0:T(8,128)(2,1)S(1)}, u32[]{:S(2)}, u32[]{:S(2)}) %all-to-all-start.3) | async-done | bytes 1572896 | tf_op jit(solution)/shard_map/all_to_all | solution.py:319
  124.4 1.7 %shard_map.149 = (bf16[256,512]{1,0:T(8,128)(2,1)}, bf16[256,512]{1,0:T(8,128)(2,1)}, f32[256,2048]{1,0:T(8,128)}) custom-call(s32[1]{0:T(128)} %bitcast.7.dp_ref, bf16[16,48,1024]{2,1,0:T(8,128)(2,1)S(1)} %all-to-all-done.3.all_ref, bf16[256,512]{1,0:T(8,128)(2,1)S(1)} %bitcast.23, bf16[256,512]{1,0:T(8,128)(2,1)S(1)} %bitcast.25), custom_call_target="tpu_custom_call" | custom-call | flops 600000000 | bytes 5000000 | tf_op jit(solution)/shard_map/pallas_call | solution.py:385
  (12 shorter events, 0.0 us)
Async XLA Ops:
  0.6 9.0 %copy-start.3 = (bf16[1,256,512]{2,1,0:T(8,128)(2,1)S(1)}, bf16[1,256,512]{2,1,0:T(8,128)(2,1)}, u32[]{:S(2)}) copy-start(bf16[1,256,512]{2,1,0:T(8,128)(2,1)} %param.15) | copy-start | bytes 786436
  2.6 35.4 %all-to-all-start = ((f32[16,16,512]{2,1,0:T(8,128)}), f32[16,16,512]{2,1,0:T(8,128)S(1)}, u32[]{:S(2)}, u32[]{:S(2)}) async-start(f32[16,16,512]{2,1,0:T(8,128)} %mix.1), calls=%async_computation | async-start | bytes 1048576 | tf_op jit(solution)/shard_map/all_to_all | solution.py:319
  9.6 15.4 %collective-permute-start = (bf16[256,512]{1,0:T(8,128)(2,1)S(1)}, bf16[256,512]{1,0:T(8,128)(2,1)S(1)}, u32[]{:S(2)}, u32[]{:S(2)}) collective-permute-start(bf16[256,512]{1,0:T(8,128)(2,1)S(1)} %bitcast.17), channel_id=1, source_target_pairs={{0,32},{16,48},{32,64},{48,80},{64,96},{80,112},{96,0},{112,16},{1... | collective-permute-start | bytes 786440 | tf_op jit(solution)/shard_map/ppermute | solution.py:301
  14.2 15.5 %collective-permute-start.1 = (bf16[256,512]{1,0:T(8,128)(2,1)S(1)}, bf16[256,512]{1,0:T(8,128)(2,1)S(1)}, u32[]{:S(2)}, u32[]{:S(2)}) collective-permute-start(bf16[256,512]{1,0:T(8,128)(2,1)S(1)} %bitcast.18), channel_id=1, source_target_pairs={{0,96},{16,112},{32,0},{48,16},{64,32},{80,48},{96,64},{112,80},{1... | collective-permute-start | bytes 786440 | tf_op jit(solution)/shard_map/ppermute | solution.py:301
  25.0 9.1 %collective-permute-start.2 = (bf16[128,512]{1,0:T(8,128)(2,1)S(1)}, bf16[128,512]{1,0:T(8,128)(2,1)S(1)}, u32[]{:S(2)}, u32[]{:S(2)}) collective-permute-start(bf16[128,512]{1,0:T(8,128)(2,1)S(1)} %slice.16), channel_id=1, source_target_pairs={{0,32},{16,48},{32,64},{48,80},{64,96},{80,112},{96,0},{112,16},{1... | collective-permute-start | bytes 393224 | tf_op jit(solution)/shard_map/ppermute | solution.py:301
  29.7 8.3 %collective-permute-start.3 = (bf16[128,512]{1,0:T(8,128)(2,1)S(1)}, bf16[128,512]{1,0:T(8,128)(2,1)S(1)}, u32[]{:S(2)}, u32[]{:S(2)}) collective-permute-start(bf16[128,512]{1,0:T(8,128)(2,1)S(1)} %slice.17), channel_id=1, source_target_pairs={{0,96},{16,112},{32,0},{48,16},{64,32},{80,48},{96,64},{112,80},{1... | collective-permute-start | bytes 393224 | tf_op jit(solution)/shard_map/ppermute | solution.py:301
  29.8 13.4 %collective-permute-start.4 = (bf16[256,512]{1,0:T(8,128)(2,1)S(1)}, bf16[256,512]{1,0:T(8,128)(2,1)S(1)}, u32[]{:S(2)}, u32[]{:S(2)}) collective-permute-start(bf16[256,512]{1,0:T(8,128)(2,1)S(1)} %bitcast.19), channel_id=1, source_target_pairs={{0,16},{16,0},{32,48},{48,32},{64,80},{80,64},{96,112},{112,96},{1... | collective-permute-start | bytes 786440 | tf_op jit(solution)/shard_map/ppermute | solution.py:301
  29.9 13.3 %copy-start.2 = (bf16[1,256,512]{2,1,0:T(8,128)(2,1)S(1)}, bf16[1,256,512]{2,1,0:T(8,128)(2,1)}, u32[]{:S(2)}) copy-start(bf16[1,256,512]{2,1,0:T(8,128)(2,1)} %param.12) | copy-start | bytes 786436
  29.9 13.3 %collective-permute-start.5 = (bf16[256,512]{1,0:T(8,128)(2,1)S(1)}, bf16[256,512]{1,0:T(8,128)(2,1)S(1)}, u32[]{:S(2)}, u32[]{:S(2)}) collective-permute-start(bf16[256,512]{1,0:T(8,128)(2,1)S(1)} %collective-permute-done.refs_1_), channel_id=1, source_target_pairs={{0,16},{16,0},{32,48},{48,32},{64,80},{80,64},{96,112},{112,96},{1... | collective-permute-start | bytes 786440 | tf_op jit(solution)/shard_map/ppermute | solution.py:301
  30.4 12.8 %collective-permute-start.6 = (bf16[256,512]{1,0:T(8,128)(2,1)S(1)}, bf16[256,512]{1,0:T(8,128)(2,1)S(1)}, u32[]{:S(2)}, u32[]{:S(2)}) collective-permute-start(bf16[256,512]{1,0:T(8,128)(2,1)S(1)} %collective-permute-done.1.refs_2_), channel_id=1, source_target_pairs={{0,16},{16,0},{32,48},{48,32},{64,80},{80,64},{96,112},{112,96},{1... | collective-permute-start | bytes 786440 | tf_op jit(solution)/shard_map/ppermute | solution.py:301
  34.1 9.1 %collective-permute-start.7 = (bf16[128,512]{1,0:T(8,128)(2,1)S(1)}, bf16[128,512]{1,0:T(8,128)(2,1)S(1)}, u32[]{:S(2)}, u32[]{:S(2)}) collective-permute-start(bf16[128,512]{1,0:T(8,128)(2,1)S(1)} %collective-permute-done.2.refs_3_), channel_id=1, source_target_pairs={{0,16},{16,0},{32,48},{48,32},{64,80},{80,64},{96,112},{112,96},{1... | collective-permute-start | bytes 393224 | tf_op jit(solution)/shard_map/ppermute | solution.py:301
  38.0 5.2 %collective-permute-start.8 = (bf16[128,512]{1,0:T(8,128)(2,1)S(1)}, bf16[128,512]{1,0:T(8,128)(2,1)S(1)}, u32[]{:S(2)}, u32[]{:S(2)}) collective-permute-start(bf16[128,512]{1,0:T(8,128)(2,1)S(1)} %collective-permute-done.3.refs_4_), channel_id=1, source_target_pairs={{0,16},{16,0},{32,48},{48,32},{64,80},{80,64},{96,112},{112,96},{1... | collective-permute-start | bytes 393224 | tf_op jit(solution)/shard_map/ppermute | solution.py:301
  42.4 0.8 copy-start.5
  43.2 3.3 %copy-start.10 = (f32[1,1024,256]{2,1,0:T(8,128)}, f32[1,1024,256]{2,1,0:T(8,128)S(1)}, u32[]{:S(2)}) copy-start(f32[1,1024,256]{2,1,0:T(8,128)S(1)} %get-tuple-element.14.spec_ref) | copy-start | bytes 3145732
  43.2 1.6 %copy-start.4 = (bf16[256,2048]{1,0:T(8,128)(2,1)S(1)}, bf16[256,2048]{1,0:T(8,128)(2,1)}, u32[]{:S(2)}) copy-start(bf16[256,2048]{1,0:T(8,128)(2,1)} %weight_ref.1) | copy-start | bytes 3145732
  46.5 22.8 %copy-start.6 = (f32[256,512]{1,0:T(8,128)}, f32[256,512]{1,0:T(8,128)S(1)}, u32[]{:S(2)}) copy-start(f32[256,512]{1,0:T(8,128)S(1)} %get-tuple-element.12) | copy-start | bytes 1572868
  68.3 1.0 copy-start
  89.0 6.7 %collective-permute-start.9 = (bf16[16,1024]{1,0:T(8,128)(2,1)S(1)}, bf16[16,1024]{1,0:T(8,128)(2,1)S(1)}, u32[]{:S(2)}, u32[]{:S(2)}) collective-permute-start(bf16[16,1024]{1,0:T(8,128)(2,1)S(1)} %total.1.mine_ref), channel_id=1, source_target_pairs={{0,128},{128,0},{1,129},{129,1},{2,130},{130,2},{3,131},{131,3},{4... | collective-permute-start | bytes 98312 | tf_op jit(solution)/shard_map/ppermute | solution.py:371
  96.9 4.2 %copy-start.1 = (bf16[16,16,1536]{2,1,0:T(8,128)(2,1)S(1)}, bf16[16,16,1536]{2,1,0:T(8,128)(2,1)}, u32[]{:S(2)}) copy-start(bf16[16,16,1536]{2,1,0:T(8,128)(2,1)} %copy-done) | copy-start | bytes 2359300
  96.9 4.2 %copy-start.7 = (f32[256,512]{1,0:T(8,128)S(1)}, f32[256,512]{1,0:T(8,128)}, u32[]{:S(2)}) copy-start(f32[256,512]{1,0:T(8,128)} %copy-done.6) | copy-start | bytes 1572868
  96.9 27.5 %all-to-all-start.3 = ((bf16[16,48,1024]{2,1,0:T(8,128)(2,1)}), bf16[16,48,1024]{2,1,0:T(8,128)(2,1)S(1)}, u32[]{:S(2)}, u32[]{:S(2)}) async-start(bf16[16,48,1024]{2,1,0:T(8,128)(2,1)} %last.1), calls=%async_computation.3 | async-start | bytes 3145728 | tf_op jit(solution)/shard_map/all_to_all | solution.py:319
  101.1 23.4 %copy-start.8 = (bf16[1,256,512]{2,1,0:T(8,128)(2,1)S(1)}, bf16[1,256,512]{2,1,0:T(8,128)(2,1)}, u32[]{:S(2)}) copy-start(bf16[1,256,512]{2,1,0:T(8,128)(2,1)} %param.13) | copy-start | bytes 786436
  101.1 23.4 %copy-start.9 = (bf16[1,256,512]{2,1,0:T(8,128)(2,1)S(1)}, bf16[1,256,512]{2,1,0:T(8,128)(2,1)}, u32[]{:S(2)}) copy-start(bf16[1,256,512]{2,1,0:T(8,128)(2,1)} %param.14) | copy-start | bytes 786436

commit v3 on v1

--- a/solution.py
+++ b/solution.py
@@ -13,7 +13,7 @@
 WIDE = 128
 TALL = 64
 LIMIT = 20
-BATCH = 8
+BATCH = 16
 
 
 def split_table(values):
@@ -131,13 +131,16 @@
             out_ref[:, m, :] = sent_rows(result, which, blocks)
 
 
-def correlate_kernel(signal_ref, spec_ref, analyse_ref, restore_ref, twist_ref, there_ref, back_ref, out_ref, rows_ref):
+def correlate_kernel(arrived_ref, spec_ref, analyse_ref, restore_ref, twist_ref, there_ref, back_ref, out_ref, signal_ref, rows_ref):
     twist = twist_ref[...]
     blocks, channels, width = rows_ref.shape
     below = out_ref.shape[1] - channels
+    both = arrived_ref[:, below:, :].astype(jnp.float32)
+    signal_ref[:, : channels // 2, :] = both[:, :, :width]
+    signal_ref[:, channels // 2 :, :] = both[:, :, width:]
     for group in range(channels // BATCH):
         members = range(group * BATCH, (group + 1) * BATCH)
-        inputs = [arrived_rows(signal_ref, m, width, width) for m in members]
+        inputs = [arrived_rows(signal_ref, m, 0, width) for m in members]
         spec = forward_group(inputs, analyse_ref[...], twist, there_ref[...])
         result = inverse_group(product(spec, spec_ref[group], True), restore_ref[...], twist, back_ref[...])
         for which, m in enumerate(members):
@@ -166,75 +169,65 @@
     out_ref[...] = mixed.reshape(out_ref.shape)
 
 
-def gate_kernel(place_ref, conv_ref, query_ref, weight_ref, *refs):
-    blocks, (both_ref, mid_ref, sem) = refs[:10], refs[10:]
+def middle_kernel(place_ref, conv_ref, query_ref, weight_ref, *refs):
+    blocks, (send_ref, grad_ref) = refs[:10], refs[10:]
     step = blocks[0].shape[0]
-    seqs, rows, width = conv_ref.shape
-    copy = pltpu.make_async_copy(conv_ref, both_ref.at[:, :, :width], sem)
-    copy.start()
+    channels, width = query_ref.shape
+    seqs, _, half = send_ref.shape
+    rows = channels // seqs
+    query = query_ref[...].astype(jnp.float32)
+    conv_out = conv_ref[...]
+    gated = (query * conv_out).astype(jnp.bfloat16)
     total = None
     for (start, size), block in zip(places(place_ref, step), blocks):
         columns = weight_ref[:, pl.ds(pl.multiple_of(start, WIDE), size)]
         term = dot(columns, block[...])
         total = term if total is None else total + term
-    mid_ref[...] = total
-    gate = query_ref[...].astype(jnp.float32) * total
-    both_ref[:, :, width:] = gate.reshape(seqs, rows, width)
-    copy.wait()
-
-
-def part_kernel(place_ref, both_ref, query_ref, *refs):
-    blocks, (part_ref,) = refs[:10], refs[10:]
-    step = blocks[0].shape[0]
-    channels, width = query_ref.shape
-    conv_out = both_ref[:, :, :width].reshape(channels, width)
-    gated = (query_ref[...].astype(jnp.float32) * conv_out).astype(jnp.bfloat16)
-    for (start, size), block in zip(places(place_ref, step), blocks):
-        term = lax.dot_general(
+        part = lax.dot_general(
             gated, block[...], (((1,), (1,)), ((), ())), preferred_element_type=jnp.float32
         )
-        part_ref[:, pl.ds(pl.multiple_of(start, WIDE), size)] = term.astype(jnp.bfloat16)
-
-
-def total_kernel(scale, part_ref, out_ref):
-    group, rows, features = part_ref.shape
-    half = features // 2
-    total = part_ref[0].astype(jnp.float32)
-    for source in range(1, group):
-        total = total + part_ref[source].astype(jnp.float32)
-    total = (total * scale).astype(jnp.bfloat16)
-    out_ref[:rows, :] = total[:, :half]
-    out_ref[rows:, :] = total[:, half:]
-
-
-def last_kernel(mine_ref, other_ref, back_ref, out_ref, sems):
+        upper = pl.multiple_of(start // half * rows, rows)
+        lane = pl.multiple_of(lax.rem(start, half), WIDE)
+        send_ref[:, pl.ds(upper, rows), pl.ds(lane, size)] = part.astype(jnp.bfloat16).reshape(
+            seqs, rows, size
+        )
+    grad_ref[...] = (total * conv_out).astype(jnp.bfloat16)
+    gate = (query * total).astype(jnp.bfloat16).reshape(seqs, rows, width)
+    send_ref[:, 2 * rows :, :width] = gate[:, : rows // 2]
+    send_ref[:, 2 * rows :, width:] = gate[:, rows // 2 :]
+
+
+def total_kernel(arrived_ref, out_ref):
+    rows = out_ref.shape[0]
+    total = arrived_ref[0, :rows, :].astype(jnp.float32)
+    for source in range(1, arrived_ref.shape[0]):
+        total = total + arrived_ref[source, :rows, :].astype(jnp.float32)
+    out_ref[...] = total
+
+
+def last_kernel(scale, mine_ref, other_ref, back_ref, out_ref, sums_ref, sems):
     rows = mine_ref.shape[0]
-    copies = []
-    for target in range(out_ref.shape[0]):
-        for turn, source in enumerate((mine_ref, other_ref)):
-            place = out_ref.at[target, turn * rows : (turn + 1) * rows, :]
-            copies.append(pltpu.make_async_copy(source, place, sems.at[target, turn]))
+    sums_ref[...] = ((mine_ref[...] + other_ref[...]) * scale).astype(jnp.bfloat16)
+    copies = [
+        pltpu.make_async_copy(sums_ref, out_ref.at[target, :rows, :], sems.at[target])
+        for target in range(out_ref.shape[0])
+    ]
     for copy in copies:
         copy.start()
     for copy in copies:
         copy.wait()
 
 
-def final_kernel(dp_ref, all_ref, key_ref, value_ref, grad_key_ref, grad_value_ref, grad_weight_ref):
+def final_kernel(all_ref, key_ref, value_ref, grad_key_ref, grad_value_ref, grad_weight_ref):
     seqs, _, half = all_ref.shape
     channels, span = key_ref.shape
-    rows = channels // (2 * seqs)
-    lanes = channels // seqs
+    rows = channels // seqs
     for source in range(seqs):
-        for turn in range(2):
-            owner = dp_ref[0] + turn - 2 * turn * dp_ref[0]
-            place = pl.ds(pl.multiple_of(owner * (channels // 2) + source * rows, 8), rows)
-            piece = all_ref[source, 2 * turn * rows : 2 * (turn + 1) * rows, :].astype(jnp.float32)
-            grad_weight_ref[place, :half] = piece[:rows]
-            grad_weight_ref[place, half:] = piece[rows:]
-        both = all_ref[source, 4 * rows :, :].astype(jnp.float32)
-        mixed = both[:, :span] + both[:, span:]
-        place = slice(source * lanes, (source + 1) * lanes)
+        piece = all_ref[source].astype(jnp.float32)
+        place = slice(source * rows, (source + 1) * rows)
+        grad_weight_ref[place, :half] = piece[:rows]
+        grad_weight_ref[place, half:] = piece[rows : 2 * rows]
+        mixed = piece[2 * rows :, :span] + piece[2 * rows :, span:]
         grad_key_ref[place, :] = (mixed * value_ref[place, :].astype(jnp.float32)).astype(jnp.bfloat16)
         grad_value_ref[place, :] = (mixed * key_ref[place, :].astype(jnp.float32)).astype(jnp.bfloat16)
 
@@ -257,29 +250,17 @@
     )(signal, filt, natural, *tables)
 
 
-def correlate(both, spec, tables, above):
-    blocks, channels, double = both.shape
+def correlate(arrived, spec, tables):
+    blocks, depth, double = arrived.shape
+    channels = depth * 2 // 5
+    shape = (blocks, channels, double // 2)
     return pl.pallas_call(
         correlate_kernel,
-        out_shape=jax.ShapeDtypeStruct((blocks, above + channels, double), jnp.bfloat16),
-        scratch_shapes=[pltpu.VMEM((blocks, channels, double // 2), jnp.float32)],
+        out_shape=jax.ShapeDtypeStruct((blocks, 3 * channels, double), jnp.bfloat16),
+        scratch_shapes=[pltpu.VMEM(shape, jnp.float32)] * 2,
         name="correlate",
         cost_estimate=pl.CostEstimate(flops=4_000_000_000, bytes_accessed=3_000_000, transcendentals=0),
-    )(both, spec, *tables)
-
-
-def placed_call(kernel, count, out_shape, left=()):
-    whole = pl.BlockSpec(memory_space=pltpu.VMEM)
-    return pl.pallas_call(
-        kernel,
-        in_specs=[pl.BlockSpec(memory_space=pltpu.SMEM)]
-        + [pl.BlockSpec(memory_space=pltpu.HBM)] * len(left)
-        + [whole] * (count - len(left)),
-        scratch_shapes=[pltpu.SemaphoreType.DMA] * len(left),
-        out_shape=out_shape,
-        compiler_params=limited(LIMIT),
-        cost_estimate=pl.CostEstimate(flops=600_000_000, bytes_accessed=5_000_000, transcendentals=0),
-    )
+    )(arrived, spec, *tables)
 
 
 def gather_features(block, chans):
@@ -327,55 +308,53 @@
     mixed_full = swap(mixed_in)
     conv_full, spec = convolve(mixed_full, long_filter, jnp.asarray(analyse_natural), tables)
 
-    both, grad_mid = placed_call(
-        gate_kernel,
-        13,
-        (
-            jax.ShapeDtypeStruct((seqs, rows, 2 * span), jnp.float32),
-            jax.ShapeDtypeStruct((channels, span), jnp.float32),
+    conv_out = swap(conv_full).reshape(channels, span)
+    whole = pl.BlockSpec(memory_space=pltpu.VMEM)
+    shape = (seqs, 3 * rows, 2 * span)
+    send, grad_query = pl.pallas_call(
+        middle_kernel,
+        in_specs=[pl.BlockSpec(memory_space=pltpu.SMEM)] + [whole] * 13,
+        out_shape=(
+            jax.ShapeDtypeStruct((seqs, 2 * rows + rows // 2, 2 * span), jnp.bfloat16),
+            jax.ShapeDtypeStruct((channels, span), jnp.bfloat16),
         ),
-        left=(0,),
-    )(place, pltpu.with_memory_space_constraint(conv_full, pltpu.HBM), query_proj[0], out_weight, *blocks)
-    both = swap(both)
-    weight_part = placed_call(
-        part_kernel, 12, jax.ShapeDtypeStruct((channels, features), jnp.bfloat16)
-    )(place, both, query_proj[0], *blocks)
-    grad_query = (grad_mid * both[:, :, :span].reshape(channels, span)).astype(jnp.bfloat16)
-
-    group = dps * seqs
-    weight_part = swap(weight_part.reshape(group, channels // group, features), ("dp", "seq"))
-    back_full = correlate(both, spec, tables, 4 * (channels // group))
-    scale = 1.0 / math.sqrt(dps * length)
-    half = features // 2
+        name="middle",
+        compiler_params=limited(LIMIT),
+        cost_estimate=pl.CostEstimate(flops=1_200_000_000, bytes_accessed=5_000_000, transcendentals=0),
+    )(place, conv_out, query_proj[0], out_weight, *blocks)
+    arrived = swap(send)
+
     mine = pl.pallas_call(
-        lambda *refs: total_kernel(scale, *refs),
-        out_shape=jax.ShapeDtypeStruct((2 * (channels // group), half), jnp.bfloat16),
+        total_kernel,
+        out_shape=jax.ShapeDtypeStruct((2 * rows, 2 * span), jnp.float32),
         name="total",
         compiler_params=limited(LIMIT),
-    )(weight_part)
+    )(arrived)
     other = lax.ppermute(mine, "dp", [(0, 1), (1, 0)])
-    whole = pl.BlockSpec(memory_space=pltpu.VMEM)
+    back_full = correlate(arrived, spec, tables)
+    scale = 1.0 / math.sqrt(dps * length)
     left = pl.BlockSpec(memory_space=pltpu.HBM)
     last = pl.pallas_call(
-        last_kernel,
+        lambda *refs: last_kernel(scale, *refs),
         in_specs=[whole, whole, left],
         out_specs=left,
-        out_shape=jax.ShapeDtypeStruct(back_full.shape, back_full.dtype),
+        out_shape=jax.ShapeDtypeStruct(shape, jnp.bfloat16),
         input_output_aliases={2: 0},
-        scratch_shapes=[pltpu.SemaphoreType.DMA((seqs, 2))],
+        scratch_shapes=[pltpu.VMEM((2 * rows, 2 * span), jnp.bfloat16), pltpu.SemaphoreType.DMA((seqs,))],
         name="last",
         compiler_params=limited(LIMIT),
     )(mine, other, pltpu.with_memory_space_constraint(back_full, pltpu.HBM))
     last = swap(last)
-    grad_key, grad_value, grad_weight = placed_call(
+    grad_key, grad_value, grad_weight = pl.pallas_call(
         final_kernel,
-        3,
-        (
+        out_shape=(
             jax.ShapeDtypeStruct((channels, span), jnp.bfloat16),
             jax.ShapeDtypeStruct((channels, span), jnp.bfloat16),
             jax.ShapeDtypeStruct((channels, features), jnp.float32),
         ),
-    )(lax.axis_index("dp").astype(jnp.int32).reshape(1), last, key_proj[0], value_proj[0])
+        name="final",
+        compiler_params=limited(LIMIT),
+    )(last, key_proj[0], value_proj[0])
     return (grad_query[None], grad_key[None], grad_value[None], grad_weight)
 
 

time: 129 us -> 115 us (0.89)
  waiting for transfers between devices: 38.3 us -> 15.1 us
  blocking collectives: 43.3 us -> 51.9 us
    all_to_all x2, waiting for transfers between devices: 20 us -> 3.79 us  [swap(): return lax.all_to_all(blocks, axes, split_axis=0, concat_axis=0, tiled=True)]
    all_to_all x2, blocking collectives: 43.3 us -> 51.9 us  [swap(): return lax.all_to_all(blocks, axes, split_axis=0, concat_axis=0, tiled=True)]
    ppermute x9, waiting for transfers between devices: 18.3 us -> 11.3 us  [send(): return lax.ppermute(values, 'chan', [(k, hop(k)) for k in range(chans)])]
    ppermute x9, starting transfers between devices: 11.8 us -> 13.4 us  [send(): return lax.ppermute(values, 'chan', [(k, hop(k)) for k in range(chans)])]
    pallas_call x5 -> x4, Pallas kernels: 5.67 us -> 6.18 us  [the longest x1 3.3 us: shards(): pl.pallas_call(middle_kernel, in_specs=[pl.BlockSpec(memory_space=pltpu.S...]
  transfers between devices with their start and end apart: 12 -> 12, of which waited for: 4 -> 4; matrix products, arithmetic and copies ran while one was open for 1% -> 0% of each run, Pallas kernels for 8% -> 9%
where the time goes in v3:
time: 115 us; the launch traced here: 114 us
  blocking collectives  51.9 us (45%)
  starting transfers between devices  27.3 us (24%)
  Pallas kernels  18.5 us (16%)
  waiting for transfers between devices  15.1 us (13%)
    all_to_all x2, blocking collectives, swap(): return lax.all_to_all(blocks, axes, split_axis=0, concat_axis=0, tiled=True)  51.9 us
    ppermute x9, starting transfers between devices, send(): return lax.ppermute(values, 'chan', [(k, hop(k)) for k in range(chans)])  13.4 us
    all_to_all x2, starting transfers between devices, swap(): return lax.all_to_all(blocks, axes, split_axis=0, concat_axis=0, tiled=True)  12.4 us
    ppermute x9, waiting for transfers between devices, send(): return lax.ppermute(values, 'chan', [(k, hop(k)) for k in range(chans)])  11.3 us
    pallas_call x1, Pallas kernels, convolve(): pl.pallas_call(convolve_kernel, out_shape=(jax.ShapeDtypeStruct(signal.sh...  5.2 us
    pallas_call x1, Pallas kernels, correlate(): pl.pallas_call(correlate_kernel, out_shape=jax.ShapeDtypeStruct((blocks,...  5.18 us
    all_to_all x2, waiting for transfers between devices, swap(): return lax.all_to_all(blocks, axes, split_axis=0, concat_axis=0, tiled=True)  3.79 us
    pallas_call x1, Pallas kernels, shards(): pl.pallas_call(middle_kernel, in_specs=[pl.BlockSpec(memory_space=pltpu.S...  3.3 us
  transfers between devices with their start and end apart: 12, of which 4 were waited for; matrix products, arithmetic and copies ran while one was open for 0% of the time, Pallas kernels for 9%

profile of v3, /device:TPU:2, one launch (start us, length us, event | category | flops | bytes accessed | tf_op | source)
XLA Modules:
  0.0 114.3 jit_solution(2822486763026652442)
XLA Ops:
  0.6 0.0 copy-start.5
  0.6 1.9 %mix.1 = f32[16,16,512]{2,1,0:T(8,128)} custom-call(bf16[256,512]{1,0:T(8,128)(2,1)} %bitcast.9, bf16[256,512]{1,0:T(8,128)(2,1)} %bitcast.11), custom_call_target="tpu_custom_call" | custom-call | tf_op jit(solution)/shard_map/mix/pallas_call | solution.py:303
  2.6 7.5 %all-to-all-start = ((f32[16,16,512]{2,1,0:T(8,128)}), f32[16,16,512]{2,1,0:T(8,128)S(1)}, u32[]{:S(2)}, u32[]{:S(2)}) async-start(f32[16,16,512]{2,1,0:T(8,128)} %mix.1), calls=%async_computation | async-start | bytes 1048576 | tf_op jit(solution)/shard_map/all_to_all | solution.py:286
  10.0 0.0 copy-done.5
  10.0 6.4 %collective-permute-start.1 = (bf16[256,512]{1,0:T(8,128)(2,1)S(1)}, bf16[256,512]{1,0:T(8,128)(2,1)S(1)}, u32[]{:S(2)}, u32[]{:S(2)}) collective-permute-start(bf16[256,512]{1,0:T(8,128)(2,1)S(1)} %bitcast.15), channel_id=1, source_target_pairs={{0,96},{16,112},{32,0},{48,16},{64,32},{80,48},{96,64},{112,80},{1... | collective-permute-start | bytes 786440 | tf_op jit(solution)/shard_map/ppermute | solution.py:268
  16.4 0.0 collective-permute-start
  16.4 3.8 %all-to-all-done.signal_ref = f32[16,16,512]{2,1,0:T(8,128)S(1)} async-done(((f32[16,16,512]{2,1,0:T(8,128)}), f32[16,16,512]{2,1,0:T(8,128)S(1)}, u32[]{:S(2)}, u32[]{:S(2)}) %all-to-all-start) | async-done | bytes 524320 | tf_op jit(solution)/shard_map/all_to_all | solution.py:286
  20.2 0.0 copy-start.6
  20.2 0.8 copy-done.6
  21.0 5.2 %convolve.1 = (f32[16,16,512]{2,1,0:T(8,128)}, f32[1,1024,256]{2,1,0:T(8,128)}) custom-call(f32[16,16,512]{2,1,0:T(8,128)} %copy-done.6, f32[16,8192]{1,0:T(8,128)} %filt_ref.1, bf16[128,192]{1,0:T(8,128)(2,1)} %constant.23.clone.natural_ref, bf16[128,192]{1,0:T(8,128)(2,1)} %constant.18.clone.analyse_ref, bf16[64,384]{1,0:T(8,128)(2,1)} %constant.19.clone.restore_ref, ...), custom_call_target="tpu_custom_call" | custom-call | flops 4000000000 | bytes 3000000 | tf_op jit(solution)/shard_map/convolve/pallas_call | solution.py:241
  26.2 0.0 copy-start.3
  26.2 0.0 copy-start.4
  26.2 5.0 %all-to-all-start.1 = ((f32[16,16,512]{2,1,0:T(8,128)}), f32[16,16,512]{2,1,0:T(8,128)S(1)}, u32[]{:S(2)}, u32[]{:S(2)}) async-start(f32[16,16,512]{2,1,0:T(8,128)} %get-tuple-element.11), calls=%async_computation.1 | async-start | bytes 1048576 | tf_op jit(solution)/shard_map/all_to_all | solution.py:286
  31.2 0.0 collective-permute-start.4
  31.2 0.0 collective-permute-done.1.refs_2_
  31.2 6.4 %collective-permute-start.3 = (bf16[128,512]{1,0:T(8,128)(2,1)S(1)}, bf16[128,512]{1,0:T(8,128)(2,1)S(1)}, u32[]{:S(2)}, u32[]{:S(2)}) collective-permute-start(bf16[128,512]{1,0:T(8,128)(2,1)S(1)} %slice.9), channel_id=1, source_target_pairs={{0,96},{16,112},{32,0},{48,16},{64,32},{80,48},{96,64},{112,80},{1... | collective-permute-start | bytes 393224 | tf_op jit(solution)/shard_map/ppermute | solution.py:268
  37.6 0.0 collective-permute-done.refs_1_
  37.6 0.1 collective-permute-start.2
  37.7 0.3 collective-permute-start.6
  38.0 0.3 collective-permute-start.5
  38.3 5.5 %collective-permute-done.3.refs_4_ = bf16[128,512]{1,0:T(8,128)(2,1)S(1)} collective-permute-done((bf16[128,512]{1,0:T(8,128)(2,1)S(1)}, bf16[128,512]{1,0:T(8,128)(2,1)S(1)}, u32[]{:S(2)}, u32[]{:S(2)}) %collective-permute-start.3) | collective-permute-done | bytes 131104 | tf_op jit(solution)/shard_map/ppermute | solution.py:268
  43.8 0.0 collective-permute-start.8
  43.8 4.0 %collective-permute-done.2.refs_3_ = bf16[128,512]{1,0:T(8,128)(2,1)} collective-permute-done((bf16[128,512]{1,0:T(8,128)(2,1)S(1)}, bf16[128,512]{1,0:T(8,128)(2,1)}, u32[]{:S(2)}, u32[]{:S(2)}) %collective-permute-start.2) | collective-permute-done | bytes 131104 | tf_op jit(solution)/shard_map/ppermute | solution.py:268
  47.9 0.0 collective-permute-start.7
  47.9 0.0 collective-permute-done.4.refs_5_
  47.9 0.0 collective-permute-done.8.refs_9_
  47.9 0.0 collective-permute-done.6.refs_7_
  47.9 1.7 %collective-permute-done.7.refs_8_ = bf16[128,512]{1,0:T(8,128)(2,1)} collective-permute-done((bf16[128,512]{1,0:T(8,128)(2,1)}, bf16[128,512]{1,0:T(8,128)(2,1)}, u32[]{:S(2)}, u32[]{:S(2)}) %collective-permute-start.7) | collective-permute-done | bytes 131104 | tf_op jit(solution)/shard_map/ppermute | solution.py:268
  49.6 0.0 collective-permute-done.5.refs_6_
  49.6 0.0 all-to-all-done.1
  49.6 0.0 copy-done.3
  49.6 0.0 copy-done.4
  49.6 3.3 %middle.1 = (bf16[16,40,1024]{2,1,0:T(8,128)(2,1)S(1)}, bf16[256,512]{1,0:T(8,128)(2,1)}) custom-call(s32[1]{0:T(128)} %bitcast.place_ref, f32[256,512]{1,0:T(8,128)S(1)} %bitcast.13, bf16[256,512]{1,0:T(8,128)(2,1)S(1)} %bitcast.14, bf16[256,2048]{1,0:T(8,128)(2,1)S(1)} %copy-done.3, bf16[256,512]{1,0:T(8,128)(2,1)S(1)} %bitcast.18, ...), custom_call_target="tpu_custom_call" | custom-call | flops 1200000000 | bytes 5000000 | tf_op jit(solution)/shard_map/middle/pallas_call | solution.py:314
  52.9 26.0 %all_to_all.20.arrived_ref = bf16[16,40,1024]{2,1,0:T(8,128)(2,1)S(1)} all-to-all(bf16[16,40,1024]{2,1,0:T(8,128)(2,1)S(1)} %get-tuple-element.13), channel_id=1, replica_groups=mesh['dp'=2,'chan'=8,'seq'=16] {'seq'}, dimensions={0} | all-to-all | bytes 2621440 | tf_op jit(solution)/shard_map/all_to_all | solution.py:286
  78.9 0.0 copy-start
  78.9 0.1 total.1.refs_0_
  79.0 1.4 %collective-permute-start.9 = (f32[32,1024]{1,0:T(8,128)S(1)}, f32[32,1024]{1,0:T(8,128)S(1)}, u32[]{:S(2)}, u32[]{:S(2)}) collective-permute-start(f32[32,1024]{1,0:T(8,128)S(1)} %total.1.refs_0_), channel_id=1, source_target_pairs={{0,128},{128,0},{1,129},{129,1},{2,130},{130,2},{3,131},{131,3},{4... | collective-permute-start | bytes 393224 | tf_op jit(solution)/shard_map/ppermute | solution.py:333
  80.4 0.0 copy-done
  80.4 5.2 %correlate.1.refs_2_ = bf16[16,48,1024]{2,1,0:T(8,128)(2,1)} custom-call(bf16[16,40,1024]{2,1,0:T(8,128)(2,1)} %copy-done, f32[1,1024,256]{2,1,0:T(8,128)} %get-tuple-element.14.spec_ref, bf16[128,192]{1,0:T(8,128)(2,1)} %constant.18.clone.analyse_ref, bf16[64,384]{1,0:T(8,128)(2,1)} %constant.19.clone.restore_ref, f32[2,64,128]{2,1,0:T(8,128)} %constant.20.clone.twist_ref, ...), custom_call_target="tpu_custom_call" | custom-call | flops 4000000000 | bytes 3000000 | tf_op jit(solution)/shard_map/correlate/pallas_call | solution.py:257
  85.6 0.0 collective-permute-done.9.refs_1_
  85.6 1.1 last.1
  86.7 0.0 copy-start.1
  86.8 0.0 copy-start.2
  86.8 25.9 %all_to_all.21.all_ref = bf16[16,48,1024]{2,1,0:T(8,128)(2,1)S(1)} all-to-all(bf16[16,48,1024]{2,1,0:T(8,128)(2,1)} %last.1), channel_id=1, replica_groups=mesh['dp'=2,'chan'=8,'seq'=16] {'seq'}, dimensions={0} | all-to-all | bytes 3145728 | tf_op jit(solution)/shard_map/all_to_all | solution.py:286
  112.7 0.0 copy-done.1
  112.7 0.0 copy-done.2
  112.7 1.6 %final.1 = (bf16[256,512]{1,0:T(8,128)(2,1)}, bf16[256,512]{1,0:T(8,128)(2,1)}, f32[256,2048]{1,0:T(8,128)}) custom-call(bf16[16,48,1024]{2,1,0:T(8,128)(2,1)S(1)} %all_to_all.21.all_ref, bf16[256,512]{1,0:T(8,128)(2,1)S(1)} %bitcast.10, bf16[256,512]{1,0:T(8,128)(2,1)S(1)} %bitcast.12), custom_call_target="tpu_custom_call" | custom-call | tf_op jit(solution)/shard_map/final/pallas_call | solution.py:348
  (2 shorter events, 0.0 us)
Async XLA Ops:
  0.6 9.4 %copy-start.5 = (bf16[1,256,512]{2,1,0:T(8,128)(2,1)S(1)}, bf16[1,256,512]{2,1,0:T(8,128)(2,1)}, u32[]{:S(2)}) copy-start(bf16[1,256,512]{2,1,0:T(8,128)(2,1)} %param.15) | copy-start | bytes 786436
  2.6 17.6 %all-to-all-start = ((f32[16,16,512]{2,1,0:T(8,128)}), f32[16,16,512]{2,1,0:T(8,128)S(1)}, u32[]{:S(2)}, u32[]{:S(2)}) async-start(f32[16,16,512]{2,1,0:T(8,128)} %mix.1), calls=%async_computation | async-start | bytes 1048576 | tf_op jit(solution)/shard_map/all_to_all | solution.py:286
  10.0 21.1 %collective-permute-start.1 = (bf16[256,512]{1,0:T(8,128)(2,1)S(1)}, bf16[256,512]{1,0:T(8,128)(2,1)S(1)}, u32[]{:S(2)}, u32[]{:S(2)}) collective-permute-start(bf16[256,512]{1,0:T(8,128)(2,1)S(1)} %bitcast.15), channel_id=1, source_target_pairs={{0,96},{16,112},{32,0},{48,16},{64,32},{80,48},{96,64},{112,80},{1... | collective-permute-start | bytes 786440 | tf_op jit(solution)/shard_map/ppermute | solution.py:268
  16.4 21.2 %collective-permute-start = (bf16[256,512]{1,0:T(8,128)(2,1)S(1)}, bf16[256,512]{1,0:T(8,128)(2,1)S(1)}, u32[]{:S(2)}, u32[]{:S(2)}) collective-permute-start(bf16[256,512]{1,0:T(8,128)(2,1)S(1)} %bitcast.16), channel_id=1, source_target_pairs={{0,32},{16,48},{32,64},{48,80},{64,96},{80,112},{96,0},{112,16},{1... | collective-permute-start | bytes 786440 | tf_op jit(solution)/shard_map/ppermute | solution.py:268
  20.2 0.8 copy-start.6
  26.2 23.4 %copy-start.3 = (bf16[256,2048]{1,0:T(8,128)(2,1)S(1)}, bf16[256,2048]{1,0:T(8,128)(2,1)}, u32[]{:S(2)}) copy-start(bf16[256,2048]{1,0:T(8,128)(2,1)} %weight_ref.1) | copy-start | bytes 3145732
  26.2 23.4 %copy-start.4 = (bf16[1,256,512]{2,1,0:T(8,128)(2,1)S(1)}, bf16[1,256,512]{2,1,0:T(8,128)(2,1)}, u32[]{:S(2)}) copy-start(bf16[1,256,512]{2,1,0:T(8,128)(2,1)} %param.12) | copy-start | bytes 786436
  26.2 23.4 %all-to-all-start.1 = ((f32[16,16,512]{2,1,0:T(8,128)}), f32[16,16,512]{2,1,0:T(8,128)S(1)}, u32[]{:S(2)}, u32[]{:S(2)}) async-start(f32[16,16,512]{2,1,0:T(8,128)} %get-tuple-element.11), calls=%async_computation.1 | async-start | bytes 1048576 | tf_op jit(solution)/shard_map/all_to_all | solution.py:286
  31.2 16.7 %collective-permute-start.4 = (bf16[256,512]{1,0:T(8,128)(2,1)S(1)}, bf16[256,512]{1,0:T(8,128)(2,1)S(1)}, u32[]{:S(2)}, u32[]{:S(2)}) collective-permute-start(bf16[256,512]{1,0:T(8,128)(2,1)S(1)} %bitcast.17), channel_id=1, source_target_pairs={{0,16},{16,0},{32,48},{48,32},{64,80},{80,64},{96,112},{112,96},{1... | collective-permute-start | bytes 786440 | tf_op jit(solution)/shard_map/ppermute | solution.py:268
  31.2 12.6 %collective-permute-start.3 = (bf16[128,512]{1,0:T(8,128)(2,1)S(1)}, bf16[128,512]{1,0:T(8,128)(2,1)S(1)}, u32[]{:S(2)}, u32[]{:S(2)}) collective-permute-start(bf16[128,512]{1,0:T(8,128)(2,1)S(1)} %slice.9), channel_id=1, source_target_pairs={{0,96},{16,112},{32,0},{48,16},{64,32},{80,48},{96,64},{112,80},{1... | collective-permute-start | bytes 393224 | tf_op jit(solution)/shard_map/ppermute | solution.py:268
  37.6 10.3 %collective-permute-start.2 = (bf16[128,512]{1,0:T(8,128)(2,1)S(1)}, bf16[128,512]{1,0:T(8,128)(2,1)}, u32[]{:S(2)}, u32[]{:S(2)}) collective-permute-start(bf16[128,512]{1,0:T(8,128)(2,1)S(1)} %slice.8), channel_id=1, source_target_pairs={{0,32},{16,48},{32,64},{48,80},{64,96},{80,112},{96,0},{112,16},{1... | collective-permute-start | bytes 393224 | tf_op jit(solution)/shard_map/ppermute | solution.py:268
  37.7 10.2 %collective-permute-start.6 = (bf16[256,512]{1,0:T(8,128)(2,1)S(1)}, bf16[256,512]{1,0:T(8,128)(2,1)S(1)}, u32[]{:S(2)}, u32[]{:S(2)}) collective-permute-start(bf16[256,512]{1,0:T(8,128)(2,1)S(1)} %collective-permute-done.1.refs_2_), channel_id=1, source_target_pairs={{0,16},{16,0},{32,48},{48,32},{64,80},{80,64},{96,112},{112,96},{1... | collective-permute-start | bytes 786440 | tf_op jit(solution)/shard_map/ppermute | solution.py:268
  38.0 11.6 %collective-permute-start.5 = (bf16[256,512]{1,0:T(8,128)(2,1)S(1)}, bf16[256,512]{1,0:T(8,128)(2,1)S(1)}, u32[]{:S(2)}, u32[]{:S(2)}) collective-permute-start(bf16[256,512]{1,0:T(8,128)(2,1)S(1)} %collective-permute-done.refs_1_), channel_id=1, source_target_pairs={{0,16},{16,0},{32,48},{48,32},{64,80},{80,64},{96,112},{112,96},{1... | collective-permute-start | bytes 786440 | tf_op jit(solution)/shard_map/ppermute | solution.py:268
  43.8 4.0 %collective-permute-start.8 = (bf16[128,512]{1,0:T(8,128)(2,1)S(1)}, bf16[128,512]{1,0:T(8,128)(2,1)}, u32[]{:S(2)}, u32[]{:S(2)}) collective-permute-start(bf16[128,512]{1,0:T(8,128)(2,1)S(1)} %collective-permute-done.3.refs_4_), channel_id=1, source_target_pairs={{0,16},{16,0},{32,48},{48,32},{64,80},{80,64},{96,112},{112,96},{1... | collective-permute-start | bytes 393224 | tf_op jit(solution)/shard_map/ppermute | solution.py:268
  47.9 1.7 %collective-permute-start.7 = (bf16[128,512]{1,0:T(8,128)(2,1)}, bf16[128,512]{1,0:T(8,128)(2,1)}, u32[]{:S(2)}, u32[]{:S(2)}) collective-permute-start(bf16[128,512]{1,0:T(8,128)(2,1)} %collective-permute-done.2.refs_3_), channel_id=1, source_target_pairs={{0,16},{16,0},{32,48},{48,32},{64,80},{80,64},{96,112},{112,96},{1... | collective-permute-start | bytes 393224 | tf_op jit(solution)/shard_map/ppermute | solution.py:268
  78.9 1.6 %copy-start = (bf16[16,40,1024]{2,1,0:T(8,128)(2,1)}, bf16[16,40,1024]{2,1,0:T(8,128)(2,1)S(1)}, u32[]{:S(2)}) copy-start(bf16[16,40,1024]{2,1,0:T(8,128)(2,1)S(1)} %all_to_all.20.arrived_ref) | copy-start | bytes 3932164
  79.0 6.6 %collective-permute-start.9 = (f32[32,1024]{1,0:T(8,128)S(1)}, f32[32,1024]{1,0:T(8,128)S(1)}, u32[]{:S(2)}, u32[]{:S(2)}) collective-permute-start(f32[32,1024]{1,0:T(8,128)S(1)} %total.1.refs_0_), channel_id=1, source_target_pairs={{0,128},{128,0},{1,129},{129,1},{2,130},{130,2},{3,131},{131,3},{4... | collective-permute-start | bytes 393224 | tf_op jit(solution)/shard_map/ppermute | solution.py:333
  86.7 26.0 %copy-start.1 = (bf16[1,256,512]{2,1,0:T(8,128)(2,1)S(1)}, bf16[1,256,512]{2,1,0:T(8,128)(2,1)}, u32[]{:S(2)}) copy-start(bf16[1,256,512]{2,1,0:T(8,128)(2,1)} %param.13) | copy-start | bytes 786436
  86.8 25.9 %copy-start.2 = (bf16[1,256,512]{2,1,0:T(8,128)(2,1)S(1)}, bf16[1,256,512]{2,1,0:T(8,128)(2,1)}, u32[]{:S(2)}) copy-start(bf16[1,256,512]{2,1,0:T(8,128)(2,1)} %param.14) | copy-start | bytes 786436

commit v4 on v3

--- a/solution.py
+++ b/solution.py
@@ -134,7 +134,7 @@
 def correlate_kernel(arrived_ref, spec_ref, analyse_ref, restore_ref, twist_ref, there_ref, back_ref, out_ref, signal_ref, rows_ref):
     twist = twist_ref[...]
     blocks, channels, width = rows_ref.shape
-    below = out_ref.shape[1] - channels
+    below = arrived_ref.shape[1] - channels // 2
     both = arrived_ref[:, below:, :].astype(jnp.float32)
     signal_ref[:, : channels // 2, :] = both[:, :, :width]
     signal_ref[:, channels // 2 :, :] = both[:, :, width:]
@@ -146,8 +146,8 @@
         for which, m in enumerate(members):
             rows_ref[:, m, :] = sent_rows(result, which, blocks)
     high, low = halves(rows_ref[...])
-    out_ref[:, below:, :width] = high
-    out_ref[:, below:, width:] = low
+    out_ref[:, :, :width] = high
+    out_ref[:, :, width:] = low
 
 
 def places(place_ref, step):
@@ -205,17 +205,11 @@
     out_ref[...] = total
 
 
-def last_kernel(scale, mine_ref, other_ref, back_ref, out_ref, sums_ref, sems):
-    rows = mine_ref.shape[0]
-    sums_ref[...] = ((mine_ref[...] + other_ref[...]) * scale).astype(jnp.bfloat16)
-    copies = [
-        pltpu.make_async_copy(sums_ref, out_ref.at[target, :rows, :], sems.at[target])
-        for target in range(out_ref.shape[0])
-    ]
-    for copy in copies:
-        copy.start()
-    for copy in copies:
-        copy.wait()
+def last_kernel(scale, mine_ref, other_ref, back_ref, out_ref):
+    rows, half = mine_ref.shape
+    sums = ((mine_ref[...] + other_ref[...]) * scale).astype(jnp.bfloat16)
+    out_ref[:, :rows, :] = jnp.broadcast_to(sums[None], (out_ref.shape[0], rows, half))
+    out_ref[:, rows:, :] = back_ref[...]
 
 
 def final_kernel(all_ref, key_ref, value_ref, grad_key_ref, grad_value_ref, grad_weight_ref):
@@ -232,6 +226,10 @@
         grad_value_ref[place, :] = (mixed * key_ref[place, :].astype(jnp.float32)).astype(jnp.bfloat16)
 
 
+def fixed(values):
+    return pltpu.with_memory_space_constraint(values, pltpu.HBM)
+
+
 def limited(mebibytes):
     return pltpu.CompilerParams(vmem_limit_bytes=mebibytes * 1024 * 1024)
 
@@ -256,9 +254,10 @@
     shape = (blocks, channels, double // 2)
     return pl.pallas_call(
         correlate_kernel,
-        out_shape=jax.ShapeDtypeStruct((blocks, 3 * channels, double), jnp.bfloat16),
+        out_shape=jax.ShapeDtypeStruct((blocks, channels, double), jnp.bfloat16),
         scratch_shapes=[pltpu.VMEM(shape, jnp.float32)] * 2,
         name="correlate",
+        compiler_params=limited(LIMIT),
         cost_estimate=pl.CostEstimate(flops=4_000_000_000, bytes_accessed=3_000_000, transcendentals=0),
     )(arrived, spec, *tables)
 
@@ -296,7 +295,7 @@
     twist, there, back = make_shared()
     analyse_natural, _ = make_tables(np.arange(TALL))
     analyse, restore = make_tables(arrived)
-    tables = tuple(jnp.asarray(t) for t in (analyse, restore, twist, there, back))
+    tables = tuple(fixed(jnp.asarray(t)) for t in (analyse, restore, twist, there, back))
     place = lax.axis_index("chan").astype(jnp.int32).reshape(1)
 
     blocks = gather_features(grad_out[0], chans)
@@ -333,17 +332,14 @@
     other = lax.ppermute(mine, "dp", [(0, 1), (1, 0)])
     back_full = correlate(arrived, spec, tables)
     scale = 1.0 / math.sqrt(dps * length)
-    left = pl.BlockSpec(memory_space=pltpu.HBM)
     last = pl.pallas_call(
         lambda *refs: last_kernel(scale, *refs),
-        in_specs=[whole, whole, left],
-        out_specs=left,
+        in_specs=[whole] * 3,
+        out_specs=whole,
         out_shape=jax.ShapeDtypeStruct(shape, jnp.bfloat16),
-        input_output_aliases={2: 0},
-        scratch_shapes=[pltpu.VMEM((2 * rows, 2 * span), jnp.bfloat16), pltpu.SemaphoreType.DMA((seqs,))],
         name="last",
         compiler_params=limited(LIMIT),
-    )(mine, other, pltpu.with_memory_space_constraint(back_full, pltpu.HBM))
+    )(mine, other, back_full)
     last = swap(last)
     grad_key, grad_value, grad_weight = pl.pallas_call(
         final_kernel,

time: 115 us -> 112 us (0.974)
  Pallas kernels: 18.5 us -> 15.7 us
    pallas_call x1, Pallas kernels: 5.18 us -> 3.36 us  [correlate(): pl.pallas_call(correlate_kernel, out_shape=jax.ShapeDtypeStruct((blocks,...]
  transfers between devices with their start and end apart: 12 -> 12, of which waited for: 4 -> 5; matrix products, arithmetic and copies ran while one was open for 0% -> 0% of each run, Pallas kernels for 9% -> 8%
where the time goes in v4:
time: 112 us; the launch traced here: 111 us
  blocking collectives  51.2 us (46%)
  starting transfers between devices  27.5 us (25%)
  Pallas kernels  15.7 us (14%)
  waiting for transfers between devices  15.3 us (14%)
    all_to_all x2, blocking collectives, swap(): return lax.all_to_all(blocks, axes, split_axis=0, concat_axis=0, tiled=True)  51.2 us
    ppermute x9, starting transfers between devices, send(): return lax.ppermute(values, 'chan', [(k, hop(k)) for k in range(chans)])  13.4 us
    all_to_all x2, starting transfers between devices, swap(): return lax.all_to_all(blocks, axes, split_axis=0, concat_axis=0, tiled=True)  12.4 us
    ppermute x9, waiting for transfers between devices, send(): return lax.ppermute(values, 'chan', [(k, hop(k)) for k in range(chans)])  11.3 us
    pallas_call x1, Pallas kernels, convolve(): pl.pallas_call(convolve_kernel, out_shape=(jax.ShapeDtypeStruct(signal.sh...  5.19 us
    all_to_all x2, waiting for transfers between devices, swap(): return lax.all_to_all(blocks, axes, split_axis=0, concat_axis=0, tiled=True)  3.79 us
    pallas_call x1, Pallas kernels, correlate(): pl.pallas_call(correlate_kernel, out_shape=jax.ShapeDtypeStruct((blocks,...  3.36 us
    pallas_call x1, Pallas kernels, shards(): pl.pallas_call(middle_kernel, in_specs=[pl.BlockSpec(memory_space=pltpu.S...  3.3 us
  transfers between devices with their start and end apart: 12, of which 5 were waited for; matrix products, arithmetic and copies ran while one was open for 0% of the time, Pallas kernels for 8%

profile of v4, /device:TPU:2, one launch (start us, length us, event | category | flops | bytes accessed | tf_op | source)
XLA Modules:
  0.0 111.3 jit_solution(9268297302561074223)
XLA Ops:
  0.6 0.0 copy-start.4
  0.6 1.9 %mix.1 = f32[16,16,512]{2,1,0:T(8,128)} custom-call(bf16[256,512]{1,0:T(8,128)(2,1)} %bitcast.9, bf16[256,512]{1,0:T(8,128)(2,1)} %bitcast.11), custom_call_target="tpu_custom_call" | custom-call | tf_op jit(solution)/shard_map/mix/pallas_call | solution.py:302
  2.6 7.5 %all-to-all-start = ((f32[16,16,512]{2,1,0:T(8,128)}), f32[16,16,512]{2,1,0:T(8,128)S(1)}, u32[]{:S(2)}, u32[]{:S(2)}) async-start(f32[16,16,512]{2,1,0:T(8,128)} %mix.1), calls=%async_computation | async-start | bytes 1048576 | tf_op jit(solution)/shard_map/all_to_all | solution.py:285
  10.0 0.0 copy-done.4
  10.0 6.4 %collective-permute-start.1 = (bf16[256,512]{1,0:T(8,128)(2,1)S(1)}, bf16[256,512]{1,0:T(8,128)(2,1)S(1)}, u32[]{:S(2)}, u32[]{:S(2)}) collective-permute-start(bf16[256,512]{1,0:T(8,128)(2,1)S(1)} %bitcast.15), channel_id=1, source_target_pairs={{0,96},{16,112},{32,0},{48,16},{64,32},{80,48},{96,64},{112,80},{1... | collective-permute-start | bytes 786440 | tf_op jit(solution)/shard_map/ppermute | solution.py:267
  16.4 0.0 collective-permute-start
  16.4 3.8 %all-to-all-done.signal_ref = f32[16,16,512]{2,1,0:T(8,128)S(1)} async-done(((f32[16,16,512]{2,1,0:T(8,128)}), f32[16,16,512]{2,1,0:T(8,128)S(1)}, u32[]{:S(2)}, u32[]{:S(2)}) %all-to-all-start) | async-done | bytes 524320 | tf_op jit(solution)/shard_map/all_to_all | solution.py:285
  20.2 0.0 copy-start.6
  20.2 0.8 copy-done.6
  21.0 5.2 %convolve.1 = (f32[16,16,512]{2,1,0:T(8,128)}, f32[1,1024,256]{2,1,0:T(8,128)}) custom-call(f32[16,16,512]{2,1,0:T(8,128)} %copy-done.6, f32[16,8192]{1,0:T(8,128)} %filt_ref.1, bf16[128,192]{1,0:T(8,128)(2,1)} %constant.23.clone.natural_ref, bf16[128,192]{1,0:T(8,128)(2,1)} %constant.18.clone.analyse_ref, bf16[64,384]{1,0:T(8,128)(2,1)} %constant.19.clone.restore_ref, ...), custom_call_target="tpu_custom_call" | custom-call | flops 4000000000 | bytes 3000000 | tf_op jit(solution)/shard_map/convolve/pallas_call | solution.py:239
  26.2 0.0 copy-start.2
  26.2 0.0 copy-start.3
  26.2 5.0 %all-to-all-start.1 = ((f32[16,16,512]{2,1,0:T(8,128)}), f32[16,16,512]{2,1,0:T(8,128)S(1)}, u32[]{:S(2)}, u32[]{:S(2)}) async-start(f32[16,16,512]{2,1,0:T(8,128)} %get-tuple-element.11), calls=%async_computation.1 | async-start | bytes 1048576 | tf_op jit(solution)/shard_map/all_to_all | solution.py:285
  31.2 0.0 collective-permute-start.4
  31.2 0.0 collective-permute-done.1.refs_2_
  31.2 6.4 %collective-permute-start.3 = (bf16[128,512]{1,0:T(8,128)(2,1)S(1)}, bf16[128,512]{1,0:T(8,128)(2,1)S(1)}, u32[]{:S(2)}, u32[]{:S(2)}) collective-permute-start(bf16[128,512]{1,0:T(8,128)(2,1)S(1)} %slice.9), channel_id=1, source_target_pairs={{0,96},{16,112},{32,0},{48,16},{64,32},{80,48},{96,64},{112,80},{1... | collective-permute-start | bytes 393224 | tf_op jit(solution)/shard_map/ppermute | solution.py:267
  37.6 0.0 collective-permute-done.refs_1_
  37.6 0.1 collective-permute-start.2
  37.7 0.3 collective-permute-start.6
  38.0 0.3 collective-permute-start.5
  38.3 5.5 %collective-permute-done.3.refs_4_ = bf16[128,512]{1,0:T(8,128)(2,1)S(1)} collective-permute-done((bf16[128,512]{1,0:T(8,128)(2,1)S(1)}, bf16[128,512]{1,0:T(8,128)(2,1)S(1)}, u32[]{:S(2)}, u32[]{:S(2)}) %collective-permute-start.3) | collective-permute-done | bytes 131104 | tf_op jit(solution)/shard_map/ppermute | solution.py:267
  43.8 0.0 collective-permute-start.8
  43.8 4.0 %collective-permute-done.2.refs_3_ = bf16[128,512]{1,0:T(8,128)(2,1)} collective-permute-done((bf16[128,512]{1,0:T(8,128)(2,1)S(1)}, bf16[128,512]{1,0:T(8,128)(2,1)}, u32[]{:S(2)}, u32[]{:S(2)}) %collective-permute-start.2) | collective-permute-done | bytes 131104 | tf_op jit(solution)/shard_map/ppermute | solution.py:267
  47.9 0.0 collective-permute-start.7
  47.9 0.0 collective-permute-done.4.refs_5_
  47.9 0.0 collective-permute-done.8.refs_9_
  47.9 0.0 collective-permute-done.6.refs_7_
  47.9 1.7 %collective-permute-done.7.refs_8_ = bf16[128,512]{1,0:T(8,128)(2,1)} collective-permute-done((bf16[128,512]{1,0:T(8,128)(2,1)}, bf16[128,512]{1,0:T(8,128)(2,1)}, u32[]{:S(2)}, u32[]{:S(2)}) %collective-permute-start.7) | collective-permute-done | bytes 131104 | tf_op jit(solution)/shard_map/ppermute | solution.py:267
  49.6 0.0 collective-permute-done.5.refs_6_
  49.6 0.0 all-to-all-done.1
  49.6 0.0 copy-done.2
  49.6 0.0 copy-done.3
  49.6 3.3 %middle.1 = (bf16[16,40,1024]{2,1,0:T(8,128)(2,1)S(1)}, bf16[256,512]{1,0:T(8,128)(2,1)}) custom-call(s32[1]{0:T(128)} %bitcast.place_ref, f32[256,512]{1,0:T(8,128)S(1)} %bitcast.13, bf16[256,512]{1,0:T(8,128)(2,1)S(1)} %bitcast.14, bf16[256,2048]{1,0:T(8,128)(2,1)S(1)} %copy-done.2, bf16[256,512]{1,0:T(8,128)(2,1)S(1)} %bitcast.18, ...), custom_call_target="tpu_custom_call" | custom-call | flops 1200000000 | bytes 5000000 | tf_op jit(solution)/shard_map/middle/pallas_call | solution.py:313
  52.9 0.0 copy-start.5
  52.9 26.1 %all_to_all.20.arrived_ref = bf16[16,40,1024]{2,1,0:T(8,128)(2,1)S(1)} all-to-all(bf16[16,40,1024]{2,1,0:T(8,128)(2,1)S(1)} %get-tuple-element.13), channel_id=1, replica_groups=mesh['dp'=2,'chan'=8,'seq'=16] {'seq'}, dimensions={0} | all-to-all | bytes 2621440 | tf_op jit(solution)/shard_map/all_to_all | solution.py:285
  79.0 0.1 total.1.refs_0_
  79.1 1.6 %collective-permute-start.9 = (f32[32,1024]{1,0:T(8,128)S(1)}, f32[32,1024]{1,0:T(8,128)S(1)}, u32[]{:S(2)}, u32[]{:S(2)}) collective-permute-start(f32[32,1024]{1,0:T(8,128)S(1)} %total.1.refs_0_), channel_id=1, source_target_pairs={{0,128},{128,0},{1,129},{129,1},{2,130},{130,2},{3,131},{131,3},{4... | collective-permute-start | bytes 393224 | tf_op jit(solution)/shard_map/ppermute | solution.py:332
  80.7 0.0 copy-done.5
  80.7 3.4 %correlate.1.refs_2_ = bf16[16,16,1024]{2,1,0:T(8,128)(2,1)S(1)} custom-call(bf16[16,40,1024]{2,1,0:T(8,128)(2,1)S(1)} %all_to_all.20.arrived_ref, f32[1,1024,256]{2,1,0:T(8,128)S(1)} %copy-done.5, bf16[128,192]{1,0:T(8,128)(2,1)} %constant.18.clone.analyse_ref, bf16[64,384]{1,0:T(8,128)(2,1)} %constant.19.clone.restore_ref, ...), custom_call_target="tpu_custom_call" | custom-call | flops 4000000000 | bytes 3000000 | tf_op jit(solution)/shard_map/correlate/pallas_call | solution.py:255
  84.1 0.2 collective-permute-done.9.refs_1_
  84.4 0.1 last.1
  84.5 0.0 copy-start
  84.5 0.0 copy-start.1
  84.5 25.1 %all_to_all.21.all_ref = bf16[16,48,1024]{2,1,0:T(8,128)(2,1)S(1)} all-to-all(bf16[16,48,1024]{2,1,0:T(8,128)(2,1)S(1)} %last.1), channel_id=1, replica_groups=mesh['dp'=2,'chan'=8,'seq'=16] {'seq'}, dimensions={0} | all-to-all | bytes 3145728 | tf_op jit(solution)/shard_map/all_to_all | solution.py:285
  109.7 0.0 copy-done
  109.7 0.0 copy-done.1
  109.7 1.6 %final.1 = (bf16[256,512]{1,0:T(8,128)(2,1)}, bf16[256,512]{1,0:T(8,128)(2,1)}, f32[256,2048]{1,0:T(8,128)}) custom-call(bf16[16,48,1024]{2,1,0:T(8,128)(2,1)S(1)} %all_to_all.21.all_ref, bf16[256,512]{1,0:T(8,128)(2,1)S(1)} %bitcast.10, bf16[256,512]{1,0:T(8,128)(2,1)S(1)} %bitcast.12), custom_call_target="tpu_custom_call" | custom-call | tf_op jit(solution)/shard_map/final/pallas_call | solution.py:344
  (2 shorter events, 0.0 us)
Async XLA Ops:
  0.6 9.4 %copy-start.4 = (bf16[1,256,512]{2,1,0:T(8,128)(2,1)S(1)}, bf16[1,256,512]{2,1,0:T(8,128)(2,1)}, u32[]{:S(2)}) copy-start(bf16[1,256,512]{2,1,0:T(8,128)(2,1)} %param.15) | copy-start | bytes 786436
  2.6 17.6 %all-to-all-start = ((f32[16,16,512]{2,1,0:T(8,128)}), f32[16,16,512]{2,1,0:T(8,128)S(1)}, u32[]{:S(2)}, u32[]{:S(2)}) async-start(f32[16,16,512]{2,1,0:T(8,128)} %mix.1), calls=%async_computation | async-start | bytes 1048576 | tf_op jit(solution)/shard_map/all_to_all | solution.py:285
  10.0 21.1 %collective-permute-start.1 = (bf16[256,512]{1,0:T(8,128)(2,1)S(1)}, bf16[256,512]{1,0:T(8,128)(2,1)S(1)}, u32[]{:S(2)}, u32[]{:S(2)}) collective-permute-start(bf16[256,512]{1,0:T(8,128)(2,1)S(1)} %bitcast.15), channel_id=1, source_target_pairs={{0,96},{16,112},{32,0},{48,16},{64,32},{80,48},{96,64},{112,80},{1... | collective-permute-start | bytes 786440 | tf_op jit(solution)/shard_map/ppermute | solution.py:267
  16.4 21.2 %collective-permute-start = (bf16[256,512]{1,0:T(8,128)(2,1)S(1)}, bf16[256,512]{1,0:T(8,128)(2,1)S(1)}, u32[]{:S(2)}, u32[]{:S(2)}) collective-permute-start(bf16[256,512]{1,0:T(8,128)(2,1)S(1)} %bitcast.16), channel_id=1, source_target_pairs={{0,32},{16,48},{32,64},{48,80},{64,96},{80,112},{96,0},{112,16},{1... | collective-permute-start | bytes 786440 | tf_op jit(solution)/shard_map/ppermute | solution.py:267
  20.2 0.8 copy-start.6
  26.2 23.4 %copy-start.2 = (bf16[256,2048]{1,0:T(8,128)(2,1)S(1)}, bf16[256,2048]{1,0:T(8,128)(2,1)}, u32[]{:S(2)}) copy-start(bf16[256,2048]{1,0:T(8,128)(2,1)} %weight_ref.1) | copy-start | bytes 3145732
  26.2 23.4 %copy-start.3 = (bf16[1,256,512]{2,1,0:T(8,128)(2,1)S(1)}, bf16[1,256,512]{2,1,0:T(8,128)(2,1)}, u32[]{:S(2)}) copy-start(bf16[1,256,512]{2,1,0:T(8,128)(2,1)} %param.12) | copy-start | bytes 786436
  26.2 23.4 %all-to-all-start.1 = ((f32[16,16,512]{2,1,0:T(8,128)}), f32[16,16,512]{2,1,0:T(8,128)S(1)}, u32[]{:S(2)}, u32[]{:S(2)}) async-start(f32[16,16,512]{2,1,0:T(8,128)} %get-tuple-element.11), calls=%async_computation.1 | async-start | bytes 1048576 | tf_op jit(solution)/shard_map/all_to_all | solution.py:285
  31.2 16.7 %collective-permute-start.4 = (bf16[256,512]{1,0:T(8,128)(2,1)S(1)}, bf16[256,512]{1,0:T(8,128)(2,1)S(1)}, u32[]{:S(2)}, u32[]{:S(2)}) collective-permute-start(bf16[256,512]{1,0:T(8,128)(2,1)S(1)} %bitcast.17), channel_id=1, source_target_pairs={{0,16},{16,0},{32,48},{48,32},{64,80},{80,64},{96,112},{112,96},{1... | collective-permute-start | bytes 786440 | tf_op jit(solution)/shard_map/ppermute | solution.py:267
  31.2 12.6 %collective-permute-start.3 = (bf16[128,512]{1,0:T(8,128)(2,1)S(1)}, bf16[128,512]{1,0:T(8,128)(2,1)S(1)}, u32[]{:S(2)}, u32[]{:S(2)}) collective-permute-start(bf16[128,512]{1,0:T(8,128)(2,1)S(1)} %slice.9), channel_id=1, source_target_pairs={{0,96},{16,112},{32,0},{48,16},{64,32},{80,48},{96,64},{112,80},{1... | collective-permute-start | bytes 393224 | tf_op jit(solution)/shard_map/ppermute | solution.py:267
  37.6 10.3 %collective-permute-start.2 = (bf16[128,512]{1,0:T(8,128)(2,1)S(1)}, bf16[128,512]{1,0:T(8,128)(2,1)}, u32[]{:S(2)}, u32[]{:S(2)}) collective-permute-start(bf16[128,512]{1,0:T(8,128)(2,1)S(1)} %slice.8), channel_id=1, source_target_pairs={{0,32},{16,48},{32,64},{48,80},{64,96},{80,112},{96,0},{112,16},{1... | collective-permute-start | bytes 393224 | tf_op jit(solution)/shard_map/ppermute | solution.py:267
  37.7 10.2 %collective-permute-start.6 = (bf16[256,512]{1,0:T(8,128)(2,1)S(1)}, bf16[256,512]{1,0:T(8,128)(2,1)S(1)}, u32[]{:S(2)}, u32[]{:S(2)}) collective-permute-start(bf16[256,512]{1,0:T(8,128)(2,1)S(1)} %collective-permute-done.1.refs_2_), channel_id=1, source_target_pairs={{0,16},{16,0},{32,48},{48,32},{64,80},{80,64},{96,112},{112,96},{1... | collective-permute-start | bytes 786440 | tf_op jit(solution)/shard_map/ppermute | solution.py:267
  38.0 11.6 %collective-permute-start.5 = (bf16[256,512]{1,0:T(8,128)(2,1)S(1)}, bf16[256,512]{1,0:T(8,128)(2,1)S(1)}, u32[]{:S(2)}, u32[]{:S(2)}) collective-permute-start(bf16[256,512]{1,0:T(8,128)(2,1)S(1)} %collective-permute-done.refs_1_), channel_id=1, source_target_pairs={{0,16},{16,0},{32,48},{48,32},{64,80},{80,64},{96,112},{112,96},{1... | collective-permute-start | bytes 786440 | tf_op jit(solution)/shard_map/ppermute | solution.py:267
  43.8 4.0 %collective-permute-start.8 = (bf16[128,512]{1,0:T(8,128)(2,1)S(1)}, bf16[128,512]{1,0:T(8,128)(2,1)}, u32[]{:S(2)}, u32[]{:S(2)}) collective-permute-start(bf16[128,512]{1,0:T(8,128)(2,1)S(1)} %collective-permute-done.3.refs_4_), channel_id=1, source_target_pairs={{0,16},{16,0},{32,48},{48,32},{64,80},{80,64},{96,112},{112,96},{1... | collective-permute-start | bytes 393224 | tf_op jit(solution)/shard_map/ppermute | solution.py:267
  47.9 1.7 %collective-permute-start.7 = (bf16[128,512]{1,0:T(8,128)(2,1)}, bf16[128,512]{1,0:T(8,128)(2,1)}, u32[]{:S(2)}, u32[]{:S(2)}) collective-permute-start(bf16[128,512]{1,0:T(8,128)(2,1)} %collective-permute-done.2.refs_3_), channel_id=1, source_target_pairs={{0,16},{16,0},{32,48},{48,32},{64,80},{80,64},{96,112},{112,96},{1... | collective-permute-start | bytes 393224 | tf_op jit(solution)/shard_map/ppermute | solution.py:267
  52.9 27.9 %copy-start.5 = (f32[1,1024,256]{2,1,0:T(8,128)S(1)}, f32[1,1024,256]{2,1,0:T(8,128)}, u32[]{:S(2)}) copy-start(f32[1,1024,256]{2,1,0:T(8,128)} %get-tuple-element.14.spec_ref) | copy-start | bytes 3145732
  79.1 5.2 %collective-permute-start.9 = (f32[32,1024]{1,0:T(8,128)S(1)}, f32[32,1024]{1,0:T(8,128)S(1)}, u32[]{:S(2)}, u32[]{:S(2)}) collective-permute-start(f32[32,1024]{1,0:T(8,128)S(1)} %total.1.refs_0_), channel_id=1, source_target_pairs={{0,128},{128,0},{1,129},{129,1},{2,130},{130,2},{3,131},{131,3},{4... | collective-permute-start | bytes 393224 | tf_op jit(solution)/shard_map/ppermute | solution.py:332
  84.5 25.2 %copy-start = (bf16[1,256,512]{2,1,0:T(8,128)(2,1)S(1)}, bf16[1,256,512]{2,1,0:T(8,128)(2,1)}, u32[]{:S(2)}) copy-start(bf16[1,256,512]{2,1,0:T(8,128)(2,1)} %param.13) | copy-start | bytes 786436
  84.5 25.1 %copy-start.1 = (bf16[1,256,512]{2,1,0:T(8,128)(2,1)S(1)}, bf16[1,256,512]{2,1,0:T(8,128)(2,1)}, u32[]{:S(2)}) copy-start(bf16[1,256,512]{2,1,0:T(8,128)(2,1)} %param.14) | copy-start | bytes 786436

commit v5 on v4

--- a/solution.py
+++ b/solution.py
@@ -71,8 +71,14 @@
     return jnp.concatenate([high, low, high], axis=1)
 
 
-def forward_group(inputs, analyse, twist, there):
-    both = dot(analyse, stacked(jnp.concatenate(inputs, axis=1)))
+def forward_group(inputs, analyse, twist, there, exact=False):
+    signal = jnp.concatenate(inputs, axis=1)
+    if exact:
+        signal = signal.astype(jnp.bfloat16)
+        analyse = jnp.concatenate([analyse[:, :TALL], analyse[:, 2 * TALL :]], axis=1)
+        both = dot(analyse, jnp.concatenate([signal, signal], axis=0))
+    else:
+        both = dot(analyse, stacked(signal))
     cos, sin = twist[0], twist[1]
     rows = []
     for which in range(len(inputs)):
@@ -141,7 +147,7 @@
     for group in range(channels // BATCH):
         members = range(group * BATCH, (group + 1) * BATCH)
         inputs = [arrived_rows(signal_ref, m, 0, width) for m in members]
-        spec = forward_group(inputs, analyse_ref[...], twist, there_ref[...])
+        spec = forward_group(inputs, analyse_ref[...], twist, there_ref[...], True)
         result = inverse_group(product(spec, spec_ref[group], True), restore_ref[...], twist, back_ref[...])
         for which, m in enumerate(members):
             rows_ref[:, m, :] = sent_rows(result, which, blocks)
@@ -303,7 +309,8 @@
         mix_kernel,
         out_shape=jax.ShapeDtypeStruct((seqs, rows, span), jnp.float32),
         name="mix",
-    )(key_proj[0], value_proj[0])
+        compiler_params=limited(LIMIT),
+    )(fixed(key_proj[0]), fixed(value_proj[0]))
     mixed_full = swap(mixed_in)
     conv_full, spec = convolve(mixed_full, long_filter, jnp.asarray(analyse_natural), tables)
 

time: 112 us -> 112 us (level)
  no operation moved by 1% of the time
where the time goes in v5:
time: 112 us; the launch traced here: 111 us
  blocking collectives  51.3 us (46%)
  starting transfers between devices  27.3 us (24%)
  Pallas kernels  15.7 us (14%)
  waiting for transfers between devices  15.3 us (14%)
    all_to_all x2, blocking collectives, swap(): return lax.all_to_all(blocks, axes, split_axis=0, concat_axis=0, tiled=True)  51.3 us
    ppermute x9, starting transfers between devices, send(): return lax.ppermute(values, 'chan', [(k, hop(k)) for k in range(chans)])  13.4 us
    all_to_all x2, starting transfers between devices, swap(): return lax.all_to_all(blocks, axes, split_axis=0, concat_axis=0, tiled=True)  12.4 us
    ppermute x9, waiting for transfers between devices, send(): return lax.ppermute(values, 'chan', [(k, hop(k)) for k in range(chans)])  11.3 us
    pallas_call x1, Pallas kernels, convolve(): pl.pallas_call(convolve_kernel, out_shape=(jax.ShapeDtypeStruct(signal.sh...  5.2 us
    all_to_all x2, waiting for transfers between devices, swap(): return lax.all_to_all(blocks, axes, split_axis=0, concat_axis=0, tiled=True)  3.79 us
    pallas_call x1, Pallas kernels, correlate(): pl.pallas_call(correlate_kernel, out_shape=jax.ShapeDtypeStruct((blocks,...  3.4 us
    pallas_call x1, Pallas kernels, shards(): pl.pallas_call(middle_kernel, in_specs=[pl.BlockSpec(memory_space=pltpu.S...  3.3 us
  transfers between devices with their start and end apart: 12, of which 5 were waited for; matrix products, arithmetic and copies ran while one was open for 0% of the time, Pallas kernels for 8%

profile of v5, /device:TPU:2, one launch (start us, length us, event | category | flops | bytes accessed | tf_op | source)
XLA Modules:
  0.0 111.2 jit_solution(4131139873152252380)
XLA Ops:
  0.6 0.0 copy-start.4
  0.6 1.9 %mix.1 = f32[16,16,512]{2,1,0:T(8,128)} custom-call(bf16[256,512]{1,0:T(8,128)(2,1)} %bitcast.9, bf16[256,512]{1,0:T(8,128)(2,1)} %bitcast.11), custom_call_target="tpu_custom_call" | custom-call | tf_op jit(solution)/shard_map/mix/pallas_call | solution.py:308
  2.6 7.5 %all-to-all-start = ((f32[16,16,512]{2,1,0:T(8,128)}), f32[16,16,512]{2,1,0:T(8,128)S(1)}, u32[]{:S(2)}, u32[]{:S(2)}) async-start(f32[16,16,512]{2,1,0:T(8,128)} %mix.1), calls=%async_computation | async-start | bytes 1048576 | tf_op jit(solution)/shard_map/all_to_all | solution.py:291
  10.0 0.0 copy-done.4
  10.0 6.4 %collective-permute-start.1 = (bf16[256,512]{1,0:T(8,128)(2,1)S(1)}, bf16[256,512]{1,0:T(8,128)(2,1)S(1)}, u32[]{:S(2)}, u32[]{:S(2)}) collective-permute-start(bf16[256,512]{1,0:T(8,128)(2,1)S(1)} %bitcast.15), channel_id=1, source_target_pairs={{0,96},{16,112},{32,0},{48,16},{64,32},{80,48},{96,64},{112,80},{1... | collective-permute-start | bytes 786440 | tf_op jit(solution)/shard_map/ppermute | solution.py:273
  16.4 0.0 collective-permute-start
  16.4 3.8 %all-to-all-done.signal_ref = f32[16,16,512]{2,1,0:T(8,128)S(1)} async-done(((f32[16,16,512]{2,1,0:T(8,128)}), f32[16,16,512]{2,1,0:T(8,128)S(1)}, u32[]{:S(2)}, u32[]{:S(2)}) %all-to-all-start) | async-done | bytes 524320 | tf_op jit(solution)/shard_map/all_to_all | solution.py:291
  20.2 0.0 copy-start.6
  20.2 0.8 copy-done.6
  21.0 5.2 %convolve.1 = (f32[16,16,512]{2,1,0:T(8,128)}, f32[1,1024,256]{2,1,0:T(8,128)}) custom-call(f32[16,16,512]{2,1,0:T(8,128)} %copy-done.6, f32[16,8192]{1,0:T(8,128)} %filt_ref.1, bf16[128,192]{1,0:T(8,128)(2,1)} %constant.23.clone.natural_ref, bf16[128,192]{1,0:T(8,128)(2,1)} %constant.18.clone.analyse_ref, bf16[64,384]{1,0:T(8,128)(2,1)} %constant.19.clone.restore_ref, ...), custom_call_target="tpu_custom_call" | custom-call | flops 4000000000 | bytes 3000000 | tf_op jit(solution)/shard_map/convolve/pallas_call | solution.py:245
  26.2 0.0 copy-start.2
  26.2 0.0 copy-start.3
  26.2 5.0 %all-to-all-start.1 = ((f32[16,16,512]{2,1,0:T(8,128)}), f32[16,16,512]{2,1,0:T(8,128)S(1)}, u32[]{:S(2)}, u32[]{:S(2)}) async-start(f32[16,16,512]{2,1,0:T(8,128)} %get-tuple-element.11), calls=%async_computation.1 | async-start | bytes 1048576 | tf_op jit(solution)/shard_map/all_to_all | solution.py:291
  31.2 0.0 collective-permute-start.4
  31.2 0.0 collective-permute-done.1.refs_2_
  31.2 6.4 %collective-permute-start.3 = (bf16[128,512]{1,0:T(8,128)(2,1)S(1)}, bf16[128,512]{1,0:T(8,128)(2,1)S(1)}, u32[]{:S(2)}, u32[]{:S(2)}) collective-permute-start(bf16[128,512]{1,0:T(8,128)(2,1)S(1)} %slice.9), channel_id=1, source_target_pairs={{0,96},{16,112},{32,0},{48,16},{64,32},{80,48},{96,64},{112,80},{1... | collective-permute-start | bytes 393224 | tf_op jit(solution)/shard_map/ppermute | solution.py:273
  37.6 0.0 collective-permute-done.refs_1_
  37.6 0.1 collective-permute-start.2
  37.7 0.3 collective-permute-start.6
  38.0 0.3 collective-permute-start.5
  38.3 5.5 %collective-permute-done.3.refs_4_ = bf16[128,512]{1,0:T(8,128)(2,1)S(1)} collective-permute-done((bf16[128,512]{1,0:T(8,128)(2,1)S(1)}, bf16[128,512]{1,0:T(8,128)(2,1)S(1)}, u32[]{:S(2)}, u32[]{:S(2)}) %collective-permute-start.3) | collective-permute-done | bytes 131104 | tf_op jit(solution)/shard_map/ppermute | solution.py:273
  43.8 0.0 collective-permute-start.8
  43.8 4.0 %collective-permute-done.2.refs_3_ = bf16[128,512]{1,0:T(8,128)(2,1)} collective-permute-done((bf16[128,512]{1,0:T(8,128)(2,1)S(1)}, bf16[128,512]{1,0:T(8,128)(2,1)}, u32[]{:S(2)}, u32[]{:S(2)}) %collective-permute-start.2) | collective-permute-done | bytes 131104 | tf_op jit(solution)/shard_map/ppermute | solution.py:273
  47.9 0.0 collective-permute-start.7
  47.9 0.0 collective-permute-done.4.refs_5_
  47.9 0.0 collective-permute-done.8.refs_9_
  47.9 0.0 collective-permute-done.6.refs_7_
  47.9 1.7 %collective-permute-done.7.refs_8_ = bf16[128,512]{1,0:T(8,128)(2,1)} collective-permute-done((bf16[128,512]{1,0:T(8,128)(2,1)}, bf16[128,512]{1,0:T(8,128)(2,1)}, u32[]{:S(2)}, u32[]{:S(2)}) %collective-permute-start.7) | collective-permute-done | bytes 131104 | tf_op jit(solution)/shard_map/ppermute | solution.py:273
  49.6 0.0 collective-permute-done.5.refs_6_
  49.6 0.0 all-to-all-done.1
  49.6 0.0 copy-done.2
  49.6 0.0 copy-done.3
  49.6 3.3 %middle.1 = (bf16[16,40,1024]{2,1,0:T(8,128)(2,1)S(1)}, bf16[256,512]{1,0:T(8,128)(2,1)}) custom-call(s32[1]{0:T(128)} %bitcast.place_ref, f32[256,512]{1,0:T(8,128)S(1)} %bitcast.13, bf16[256,512]{1,0:T(8,128)(2,1)S(1)} %bitcast.14, bf16[256,2048]{1,0:T(8,128)(2,1)S(1)} %copy-done.2, bf16[256,512]{1,0:T(8,128)(2,1)S(1)} %bitcast.18, ...), custom_call_target="tpu_custom_call" | custom-call | flops 1200000000 | bytes 5000000 | tf_op jit(solution)/shard_map/middle/pallas_call | solution.py:320
  52.9 0.0 copy-start.5
  52.9 26.1 %all_to_all.20.arrived_ref = bf16[16,40,1024]{2,1,0:T(8,128)(2,1)S(1)} all-to-all(bf16[16,40,1024]{2,1,0:T(8,128)(2,1)S(1)} %get-tuple-element.13), channel_id=1, replica_groups=mesh['dp'=2,'chan'=8,'seq'=16] {'seq'}, dimensions={0} | all-to-all | bytes 2621440 | tf_op jit(solution)/shard_map/all_to_all | solution.py:291
  79.0 0.1 total.1.refs_0_
  79.1 1.4 %collective-permute-start.9 = (f32[32,1024]{1,0:T(8,128)S(1)}, f32[32,1024]{1,0:T(8,128)S(1)}, u32[]{:S(2)}, u32[]{:S(2)}) collective-permute-start(f32[32,1024]{1,0:T(8,128)S(1)} %total.1.refs_0_), channel_id=1, source_target_pairs={{0,128},{128,0},{1,129},{129,1},{2,130},{130,2},{3,131},{131,3},{4... | collective-permute-start | bytes 393224 | tf_op jit(solution)/shard_map/ppermute | solution.py:339
  80.6 0.0 copy-done.5
  80.6 3.4 %correlate.1.refs_2_ = bf16[16,16,1024]{2,1,0:T(8,128)(2,1)S(1)} custom-call(bf16[16,40,1024]{2,1,0:T(8,128)(2,1)S(1)} %all_to_all.20.arrived_ref, f32[1,1024,256]{2,1,0:T(8,128)S(1)} %copy-done.5, bf16[128,192]{1,0:T(8,128)(2,1)} %constant.18.clone.analyse_ref, bf16[64,384]{1,0:T(8,128)(2,1)} %constant.19.clone.restore_ref, ...), custom_call_target="tpu_custom_call" | custom-call | flops 4000000000 | bytes 3000000 | tf_op jit(solution)/shard_map/correlate/pallas_call | solution.py:261
  84.0 0.2 collective-permute-done.9.refs_1_
  84.2 0.1 last.1
  84.3 0.0 copy-start
  84.3 0.0 copy-start.1
  84.4 25.2 %all_to_all.21.all_ref = bf16[16,48,1024]{2,1,0:T(8,128)(2,1)S(1)} all-to-all(bf16[16,48,1024]{2,1,0:T(8,128)(2,1)S(1)} %last.1), channel_id=1, replica_groups=mesh['dp'=2,'chan'=8,'seq'=16] {'seq'}, dimensions={0} | all-to-all | bytes 3145728 | tf_op jit(solution)/shard_map/all_to_all | solution.py:291
  109.5 0.0 copy-done
  109.5 0.0 copy-done.1
  109.5 1.6 %final.1 = (bf16[256,512]{1,0:T(8,128)(2,1)}, bf16[256,512]{1,0:T(8,128)(2,1)}, f32[256,2048]{1,0:T(8,128)}) custom-call(bf16[16,48,1024]{2,1,0:T(8,128)(2,1)S(1)} %all_to_all.21.all_ref, bf16[256,512]{1,0:T(8,128)(2,1)S(1)} %bitcast.10, bf16[256,512]{1,0:T(8,128)(2,1)S(1)} %bitcast.12), custom_call_target="tpu_custom_call" | custom-call | tf_op jit(solution)/shard_map/final/pallas_call | solution.py:351
  (2 shorter events, 0.0 us)
Async XLA Ops:
  0.6 9.4 %copy-start.4 = (bf16[1,256,512]{2,1,0:T(8,128)(2,1)S(1)}, bf16[1,256,512]{2,1,0:T(8,128)(2,1)}, u32[]{:S(2)}) copy-start(bf16[1,256,512]{2,1,0:T(8,128)(2,1)} %param.15) | copy-start | bytes 786436
  2.6 17.6 %all-to-all-start = ((f32[16,16,512]{2,1,0:T(8,128)}), f32[16,16,512]{2,1,0:T(8,128)S(1)}, u32[]{:S(2)}, u32[]{:S(2)}) async-start(f32[16,16,512]{2,1,0:T(8,128)} %mix.1), calls=%async_computation | async-start | bytes 1048576 | tf_op jit(solution)/shard_map/all_to_all | solution.py:291
  10.0 21.1 %collective-permute-start.1 = (bf16[256,512]{1,0:T(8,128)(2,1)S(1)}, bf16[256,512]{1,0:T(8,128)(2,1)S(1)}, u32[]{:S(2)}, u32[]{:S(2)}) collective-permute-start(bf16[256,512]{1,0:T(8,128)(2,1)S(1)} %bitcast.15), channel_id=1, source_target_pairs={{0,96},{16,112},{32,0},{48,16},{64,32},{80,48},{96,64},{112,80},{1... | collective-permute-start | bytes 786440 | tf_op jit(solution)/shard_map/ppermute | solution.py:273
  16.4 21.2 %collective-permute-start = (bf16[256,512]{1,0:T(8,128)(2,1)S(1)}, bf16[256,512]{1,0:T(8,128)(2,1)S(1)}, u32[]{:S(2)}, u32[]{:S(2)}) collective-permute-start(bf16[256,512]{1,0:T(8,128)(2,1)S(1)} %bitcast.16), channel_id=1, source_target_pairs={{0,32},{16,48},{32,64},{48,80},{64,96},{80,112},{96,0},{112,16},{1... | collective-permute-start | bytes 786440 | tf_op jit(solution)/shard_map/ppermute | solution.py:273
  20.2 0.8 copy-start.6
  26.2 23.4 %copy-start.2 = (bf16[256,2048]{1,0:T(8,128)(2,1)S(1)}, bf16[256,2048]{1,0:T(8,128)(2,1)}, u32[]{:S(2)}) copy-start(bf16[256,2048]{1,0:T(8,128)(2,1)} %weight_ref.1) | copy-start | bytes 3145732
  26.2 23.4 %copy-start.3 = (bf16[1,256,512]{2,1,0:T(8,128)(2,1)S(1)}, bf16[1,256,512]{2,1,0:T(8,128)(2,1)}, u32[]{:S(2)}) copy-start(bf16[1,256,512]{2,1,0:T(8,128)(2,1)} %param.12) | copy-start | bytes 786436
  26.2 23.4 %all-to-all-start.1 = ((f32[16,16,512]{2,1,0:T(8,128)}), f32[16,16,512]{2,1,0:T(8,128)S(1)}, u32[]{:S(2)}, u32[]{:S(2)}) async-start(f32[16,16,512]{2,1,0:T(8,128)} %get-tuple-element.11), calls=%async_computation.1 | async-start | bytes 1048576 | tf_op jit(solution)/shard_map/all_to_all | solution.py:291
  31.2 16.7 %collective-permute-start.4 = (bf16[256,512]{1,0:T(8,128)(2,1)S(1)}, bf16[256,512]{1,0:T(8,128)(2,1)S(1)}, u32[]{:S(2)}, u32[]{:S(2)}) collective-permute-start(bf16[256,512]{1,0:T(8,128)(2,1)S(1)} %bitcast.17), channel_id=1, source_target_pairs={{0,16},{16,0},{32,48},{48,32},{64,80},{80,64},{96,112},{112,96},{1... | collective-permute-start | bytes 786440 | tf_op jit(solution)/shard_map/ppermute | solution.py:273
  31.2 12.6 %collective-permute-start.3 = (bf16[128,512]{1,0:T(8,128)(2,1)S(1)}, bf16[128,512]{1,0:T(8,128)(2,1)S(1)}, u32[]{:S(2)}, u32[]{:S(2)}) collective-permute-start(bf16[128,512]{1,0:T(8,128)(2,1)S(1)} %slice.9), channel_id=1, source_target_pairs={{0,96},{16,112},{32,0},{48,16},{64,32},{80,48},{96,64},{112,80},{1... | collective-permute-start | bytes 393224 | tf_op jit(solution)/shard_map/ppermute | solution.py:273
  37.6 10.3 %collective-permute-start.2 = (bf16[128,512]{1,0:T(8,128)(2,1)S(1)}, bf16[128,512]{1,0:T(8,128)(2,1)}, u32[]{:S(2)}, u32[]{:S(2)}) collective-permute-start(bf16[128,512]{1,0:T(8,128)(2,1)S(1)} %slice.8), channel_id=1, source_target_pairs={{0,32},{16,48},{32,64},{48,80},{64,96},{80,112},{96,0},{112,16},{1... | collective-permute-start | bytes 393224 | tf_op jit(solution)/shard_map/ppermute | solution.py:273
  37.7 10.2 %collective-permute-start.6 = (bf16[256,512]{1,0:T(8,128)(2,1)S(1)}, bf16[256,512]{1,0:T(8,128)(2,1)S(1)}, u32[]{:S(2)}, u32[]{:S(2)}) collective-permute-start(bf16[256,512]{1,0:T(8,128)(2,1)S(1)} %collective-permute-done.1.refs_2_), channel_id=1, source_target_pairs={{0,16},{16,0},{32,48},{48,32},{64,80},{80,64},{96,112},{112,96},{1... | collective-permute-start | bytes 786440 | tf_op jit(solution)/shard_map/ppermute | solution.py:273
  38.0 11.6 %collective-permute-start.5 = (bf16[256,512]{1,0:T(8,128)(2,1)S(1)}, bf16[256,512]{1,0:T(8,128)(2,1)S(1)}, u32[]{:S(2)}, u32[]{:S(2)}) collective-permute-start(bf16[256,512]{1,0:T(8,128)(2,1)S(1)} %collective-permute-done.refs_1_), channel_id=1, source_target_pairs={{0,16},{16,0},{32,48},{48,32},{64,80},{80,64},{96,112},{112,96},{1... | collective-permute-start | bytes 786440 | tf_op jit(solution)/shard_map/ppermute | solution.py:273
  43.8 4.0 %collective-permute-start.8 = (bf16[128,512]{1,0:T(8,128)(2,1)S(1)}, bf16[128,512]{1,0:T(8,128)(2,1)}, u32[]{:S(2)}, u32[]{:S(2)}) collective-permute-start(bf16[128,512]{1,0:T(8,128)(2,1)S(1)} %collective-permute-done.3.refs_4_), channel_id=1, source_target_pairs={{0,16},{16,0},{32,48},{48,32},{64,80},{80,64},{96,112},{112,96},{1... | collective-permute-start | bytes 393224 | tf_op jit(solution)/shard_map/ppermute | solution.py:273
  47.9 1.7 %collective-permute-start.7 = (bf16[128,512]{1,0:T(8,128)(2,1)}, bf16[128,512]{1,0:T(8,128)(2,1)}, u32[]{:S(2)}, u32[]{:S(2)}) collective-permute-start(bf16[128,512]{1,0:T(8,128)(2,1)} %collective-permute-done.2.refs_3_), channel_id=1, source_target_pairs={{0,16},{16,0},{32,48},{48,32},{64,80},{80,64},{96,112},{112,96},{1... | collective-permute-start | bytes 393224 | tf_op jit(solution)/shard_map/ppermute | solution.py:273
  52.9 27.7 %copy-start.5 = (f32[1,1024,256]{2,1,0:T(8,128)S(1)}, f32[1,1024,256]{2,1,0:T(8,128)}, u32[]{:S(2)}) copy-start(f32[1,1024,256]{2,1,0:T(8,128)} %get-tuple-element.14.spec_ref) | copy-start | bytes 3145732
  79.1 5.1 %collective-permute-start.9 = (f32[32,1024]{1,0:T(8,128)S(1)}, f32[32,1024]{1,0:T(8,128)S(1)}, u32[]{:S(2)}, u32[]{:S(2)}) collective-permute-start(f32[32,1024]{1,0:T(8,128)S(1)} %total.1.refs_0_), channel_id=1, source_target_pairs={{0,128},{128,0},{1,129},{129,1},{2,130},{130,2},{3,131},{131,3},{4... | collective-permute-start | bytes 393224 | tf_op jit(solution)/shard_map/ppermute | solution.py:339
  84.3 25.2 %copy-start = (bf16[1,256,512]{2,1,0:T(8,128)(2,1)S(1)}, bf16[1,256,512]{2,1,0:T(8,128)(2,1)}, u32[]{:S(2)}) copy-start(bf16[1,256,512]{2,1,0:T(8,128)(2,1)} %param.13) | copy-start | bytes 786436
  84.3 25.2 %copy-start.1 = (bf16[1,256,512]{2,1,0:T(8,128)(2,1)S(1)}, bf16[1,256,512]{2,1,0:T(8,128)(2,1)}, u32[]{:S(2)}) copy-start(bf16[1,256,512]{2,1,0:T(8,128)(2,1)} %param.14) | copy-start | bytes 786436
